TPU v7x, 512 devices: a whole 4x4x16 slice. The times are simulated.
512 devices in a mesh: row: 16 (over x_lo, y, core), col: 32 (over x_hi, z).
Axes of the slice: x: 4 (x_hi: 2, x_lo: 2; x = x_hi * 2 + x_lo), y: 4, z: 16, core: 2. Of those that a mesh axis runs over, the one named last changes fastest.
Arguments:
- inverse_slab: bfloat16 [65536, 8192], P('row', 'col'), may hold values from -0.0234375 to 0.0234375
- cot_solved: bfloat16 [64, 65536], P(None, ('row', 'col')), may hold values from -6 to 6
- cot_direct: bfloat16 [64, 8192], P(None, 'col'), may hold values from -6 to 6
- solved_panel: bfloat16 [64, 65536], P(None, 'col'), may hold values from -1.078125 to 1.078125
Outputs:
- grad_factor: float32 [64, 8192], P(None, 'col')
- grad_operator: bfloat16 [8192, 65536], P('row', 'col')
All inputs are finite; a program needn't handle non-finite values.
Results may differ from a plain program's by a relative error of at most 0.0049.
Values may be sent and summed in bfloat16 or wider, within the bound.
No kernel may reach another device: no remote copies, remote signals or barrier semaphores. Data moves between devices by JAX's collectives and lax.ppermute only.
A program may use at most 64 MiB of HBM per device.

v0:
```python
import jax
import jax.numpy as jnp
from jax import lax
from jax.sharding import PartitionSpec as P


def body(inverse_slab, cot_solved, cot_direct, solved_panel):
    scale = 1.0 / jnp.sqrt(jnp.float32(2.0))
    block_rows = lax.all_gather(cot_solved, "col", axis=1, tiled=True)
    partial_sum = jnp.dot(block_rows, inverse_slab, preferred_element_type=jnp.float32)
    pulled = lax.psum(partial_sum, "row")
    grad_factor = (cot_direct.astype(jnp.float32) + pulled) * scale
    pulled_low = pulled.astype(jnp.bfloat16)
    width = pulled_low.shape[1]
    factor = lax.axis_size("col") // lax.axis_size("row")
    gathered = lax.all_gather(pulled_low, "col", axis=1, tiled=True)
    offset = lax.axis_index("row") * (factor * width)
    needed = lax.dynamic_slice_in_dim(gathered, offset, factor * width, 1)
    product = lax.dot_general(
        needed, solved_panel, (((0,), (0,)), ((), ())), preferred_element_type=jnp.float32
    )
    grad_operator = (product * -scale).astype(jnp.bfloat16)
    return (grad_factor, grad_operator)


def solution(mesh):
    in_specs = (P("row", "col"), P(None, ("row", "col")), P(None, "col"), P(None, "col"))
    out_specs = (P(None, "col"), P("row", "col"))
    return jax.shard_map(body, mesh=mesh, in_specs=in_specs, out_specs=out_specs, check_vma=False)
```

profile of v0, /device:TPU:8, one launch (start us, length us, event | category | flops | bytes accessed | tf_op | source)
XLA Modules:
  0.0 356.7 jit_solution(521984565598067549)
XLA Ops:
  7.2 0.0 copy-start
  7.2 0.0 copy-start.2
  7.2 0.0 copy-start.1
  7.2 0.0 all-reduce.2.cloned.1.call-start
  7.2 85.5 %all_gather.6 = bf16[64,4096]{1,0:T(8,128)(2,1)S(1)} all-gather(bf16[64,128]{1,0:T(8,128)(2,1)} %param.5), channel_id=1, replica_groups=mesh['row'=16,'col'=32] {'col'}, dimensions={1}, use_global_device_ids=true | all-gather | bytes 540672 | tf_op jit(solution)/shard_map/all_gather | solution.py:9
  92.8 0.0 copy-done
  92.8 1.1 fusion.3
  93.8 0.0 all-reduce.2.cloned.1.call-update
  93.9 0.0 all-gather.2.cloned.1.call-start
  93.9 111.6 %all-reduce.2.cloned.1.call-done = f32[64,256]{1,0:T(8,128)} async-done(((f32[64,256]{1,0:T(8,128)}), f32[64,256]{1,0:T(8,128)}) %all-reduce.2.cloned.1.call-update) | async-done | bytes 65552 | tf_op jit(solution)/shard_map/psum | solution.py:11
  205.6 0.0 copy-done.2
  205.6 1.6 fusion.2
  207.1 0.0 all-gather.2.cloned.1.call-update
  207.1 139.8 %all-gather.2.cloned.1.call-done = bf16[64,8192]{1,0:T(8,128)(2,1)} async-done(((bf16[64,256]{1,0:T(8,128)(2,1)}), bf16[64,8192]{1,0:T(8,128)(2,1)}) %all-gather.2.cloned.1.call-update) | async-done | bytes 1048592 | tf_op jit(solution)/shard_map/all_gather | solution.py:16
  347.0 0.0 copy-done.1
  347.0 2.9 multiply_convert_fusion
Async XLA Ops:
  7.2 85.6 %copy-start = (bf16[4096,256]{1,0:T(8,128)(2,1)S(1)}, bf16[4096,256]{1,0:T(8,128)(2,1)}, u32[]{:S(2)}) copy-start(bf16[4096,256]{1,0:T(8,128)(2,1)} %param.4) | copy-start | bytes 6291460
  7.2 198.4 %copy-start.2 = (bf16[64,256]{1,0:T(8,128)(2,1)S(1)}, bf16[64,256]{1,0:T(8,128)(2,1)}, u32[]{:S(2)}) copy-start(bf16[64,256]{1,0:T(8,128)(2,1)} %param.6) | copy-start | bytes 98308
  7.2 339.8 %copy-start.1 = (bf16[64,2048]{1,0:T(8,128)(2,1)S(1)}, bf16[64,2048]{1,0:T(8,128)(2,1)}, u32[]{:S(2)}) copy-start(bf16[64,2048]{1,0:T(8,128)(2,1)} %param.7) | copy-start | bytes 786436
  7.2 198.4 %all-reduce.2.cloned.1.call-start = ((), (), s32[]{:S(2)}) async-start(), calls=%async_computation | async-start | bytes 131072 | tf_op jit(solution)/shard_map/psum | solution.py:11
  93.9 253.1 %all-gather.2.cloned.1.call-start = ((), (), s32[]{:S(2)}) async-start(), calls=%async_computation.1 | async-start | bytes 1081344 | tf_op jit(solution)/shard_map/all_gather | solution.py:16
Sparse Core Ops, SparseCore 0:
  94.0 111.5 all-reduce.1
  209.0 137.8 all-gather.1
where the time goes:
time: 357 us
  waiting for transfers between devices  251 us (70%)
  blocking collectives  85.5 us (24%)
  between operations  14.1 us (4%)
  matrix products  3.98 us (1%)
    all_gather x1, waiting for transfers between devices, body(): gathered = lax.all_gather(pulled_low, 'col', axis=1, tiled=True)  140 us
    psum x1, waiting for transfers between devices, body(): pulled = lax.psum(partial_sum, 'row')  112 us
    all_gather x1, blocking collectives, body(): block_rows = lax.all_gather(cot_solved, 'col', axis=1, tiled=True)  85.5 us
  transfers between devices with their start and end apart: 2, of which 2 were waited for; matrix products, arithmetic and copies ran while one was open for 0% of the time, Pallas kernels for 0%

commit v1 on v0

v1 whole, which is shorter than its diff:
```python
import jax
import jax.numpy as jnp
from jax import lax
from jax.experimental import pallas as pl
from jax.experimental.pallas import tpu as pltpu
from jax.sharding import PartitionSpec as P

SUB, LANE = 8, 128
F32, BF16 = jnp.float32, jnp.bfloat16
VMEM = pltpu.VMEM


def full(shape):
    return pl.BlockSpec(shape, lambda *_: (0,) * len(shape))


def partial_kernel(blocks_ref, slab_ref, out_ref):
    n, _, b = blocks_ref.shape
    pair = 2
    total = None
    for i in range(0, n, pair):
        left = jnp.concatenate([blocks_ref[i + j] for j in range(pair)], axis=1)
        term = jnp.dot(left, slab_ref[i * b : (i + pair) * b, :], preferred_element_type=F32)
        total = term if total is None else total + term
    tiles_across = total.shape[1] // LANE
    for t in range(out_ref.shape[0]):
        i, j = t // tiles_across, t % tiles_across
        out_ref[t] = total[i * SUB : (i + 1) * SUB, j * LANE : (j + 1) * LANE]


def partial_tiles(blocks, slab):
    n, k, b = blocks.shape
    tiles = (k // SUB) * (slab.shape[1] // LANE)
    return pl.pallas_call(
        partial_kernel,
        out_shape=jax.ShapeDtypeStruct((tiles, SUB, LANE), F32),
        cost_estimate=pl.CostEstimate(
            flops=2 * n * k * b * slab.shape[1],
            bytes_accessed=2 * (blocks.size + slab.size) + 4 * tiles * SUB * LANE,
            transcendentals=0,
        ),
    )(blocks, slab)


def reduced_kernel(tiles_ref, high_ref, own_ref):
    pulled = tiles_ref[0]
    for t in range(1, tiles_ref.shape[0]):
        pulled = pulled + tiles_ref[t]
    high = pulled.astype(BF16)
    low = (pulled - high.astype(F32)).astype(BF16)
    for t in range(high_ref.shape[0]):
        high_ref[t] = high
    for t in range(own_ref.shape[0]):
        own_ref[t, 0] = high
        own_ref[t, 1] = low


def reduced(tiles, copies):
    rows = tiles.shape[0]
    tile = tiles.shape[1:]
    return pl.pallas_call(
        reduced_kernel,
        out_shape=[
            jax.ShapeDtypeStruct((copies,) + tile, BF16),
            jax.ShapeDtypeStruct((rows, 2) + tile, BF16),
        ],
        cost_estimate=pl.CostEstimate(
            flops=tiles.size, bytes_accessed=4 * tiles.size + 2 * (copies + 2 * rows) * SUB * LANE, transcendentals=0
        ),
    )(tiles)


def product_kernel(scale, tiles_ref, direct_ref, panel_ref, factor_ref, out_ref, left_ref):
    rows = tiles_ref.shape[0]
    width = direct_ref.shape[1]
    across = width // LANE
    chunk = out_ref.shape[0]

    @pl.when(pl.program_id(0) == 0)
    def _():
        for t in range(rows):
            i, j = t // across, t % across
            at = slice(i * SUB, (i + 1) * SUB)
            for b in range(2):
                lane = (b * across + j) * LANE
                left_ref[lane // chunk, at, lane % chunk : lane % chunk + LANE] = tiles_ref[t, b].astype(F32)
            lanes = slice(j * LANE, (j + 1) * LANE)
            pulled = tiles_ref[t, 2].astype(F32) + tiles_ref[t, 3].astype(F32)
            factor_ref[at, lanes] = (direct_ref[at, lanes].astype(F32) + pulled) * scale

    left = left_ref[pl.program_id(0)].astype(BF16)
    product = lax.dot_general(left, panel_ref[...], (((0,), (0,)), ((), ())), preferred_element_type=F32)
    out_ref[...] = (product * -scale).astype(BF16)


def products(tiles, direct, panel, scale):
    k, width = direct.shape
    depth = 2 * width
    chunk = depth // 4
    columns = panel.shape[1]

    def kernel(*refs):
        product_kernel(scale, *refs)

    return pl.pallas_call(
        kernel,
        grid=(depth // chunk,),
        in_specs=[full(tiles.shape), full(direct.shape), full(panel.shape)],
        out_specs=[full((k, width)), pl.BlockSpec((chunk, columns), lambda i: (i, 0))],
        out_shape=[
            jax.ShapeDtypeStruct((k, width), F32),
            jax.ShapeDtypeStruct((depth, columns), BF16),
        ],
        scratch_shapes=[VMEM((depth // chunk, k, chunk), F32)],
        cost_estimate=pl.CostEstimate(
            flops=2 * k * depth * columns,
            bytes_accessed=2 * (depth * columns + panel.size + tiles.size),
            transcendentals=0,
        ),
    )(tiles, direct, panel)


def body(inverse_slab, cot_solved, cot_direct, solved_panel):
    scale = 0.5 ** 0.5
    rows, cols = lax.axis_size("row"), lax.axis_size("col")
    blocks = lax.all_to_all(
        jnp.broadcast_to(cot_solved, (cols,) + cot_solved.shape), "col", 0, 0, tiled=True
    )
    tiles = partial_tiles(blocks, inverse_slab)
    high, own = reduced(lax.all_to_all(tiles, "row", 0, 0, tiled=True), cols)
    every = lax.all_to_all(high, "col", 0, 0, tiled=True)
    sent = jnp.concatenate([every.reshape((rows, cols // rows) + high.shape[1:]), own], axis=1)
    needed = lax.all_to_all(sent, "row", 0, 0, tiled=True)
    return tuple(products(needed, cot_direct, solved_panel, scale))


def solution(mesh):
    in_specs = (P("row", "col"), P(None, ("row", "col")), P(None, "col"), P(None, "col"))
    out_specs = (P(None, "col"), P("row", "col"))
    return jax.shard_map(body, mesh=mesh, in_specs=in_specs, out_specs=out_specs, check_vma=False)
```

time: 357 us -> 105 us (0.29)
  the two profiles are of different devices: /device:TPU:8 before, /device:TPU:1 now
where the time goes in v1:
time: 105 us; the launch traced here: 104 us
  blocking collectives  94 us (90%)
  Pallas kernels  8.02 us (8%)
    all_to_all x1, blocking collectives, body(): lax.all_to_all(jnp.broadcast_to(cot_solved, (cols,) + cot_solved.shape),...  50.5 us
    all_to_all x1, blocking collectives, body(): every = lax.all_to_all(high, 'col', 0, 0, tiled=True)  20.1 us
    all_to_all x1, blocking collectives, body(): high, own = reduced(lax.all_to_all(tiles, 'row', 0, 0, tiled=True), cols)  11.9 us
    all_to_all x1, blocking collectives, body(): needed = lax.all_to_all(sent, 'row', 0, 0, tiled=True)  11.4 us
    pallas_call x1, Pallas kernels, products(): pl.pallas_call(kernel, grid=(depth // chunk,), in_specs=[full(tiles.shape...  3.63 us
    pallas_call x1, Pallas kernels, partial_tiles(): pl.pallas_call(partial_kernel, out_shape=jax.ShapeDtypeStruct((tiles, SUB...  2.88 us

profile of v1, /device:TPU:1, one launch (start us, length us, event | category | flops | bytes accessed | tf_op | source)
XLA Modules:
  0.0 104.4 jit_solution(6834848573612800686)
XLA Ops:
  0.6 0.8 broadcast_in_dim.3
  1.5 50.5 %all_to_all.20.blocks_ref = bf16[32,64,128]{2,1,0:T(8,128)(2,1)} all-to-all(bf16[32,64,128]{2,1,0:T(8,128)(2,1)S(1)} %broadcast_in_dim.3), channel_id=1, replica_groups=mesh['row'=16,'col'=32] {'col'}, dimensions={0} | all-to-all | bytes 1048576 | tf_op jit(solution)/shard_map/all_to_all | solution.py:126
  52.0 2.9 %shard_map.59 = f32[16,8,128]{2,1,0:T(8,128)} custom-call(bf16[32,64,128]{2,1,0:T(8,128)(2,1)} %all_to_all.20.blocks_ref, bf16[4096,256]{1,0:T(8,128)(2,1)} %slab_ref.1), custom_call_target="tpu_custom_call" | custom-call | flops 134217728 | bytes 2686976 | tf_op jit(solution)/shard_map/pallas_call | solution.py:34
  54.9 11.9 %all_to_all.21.tiles_ref = f32[16,8,128]{2,1,0:T(8,128)} all-to-all(f32[16,8,128]{2,1,0:T(8,128)} %shard_map.59), channel_id=1, replica_groups=mesh['row'=16,'col'=32] {'row'}, dimensions={0} | all-to-all | bytes 131072 | tf_op jit(solution)/shard_map/all_to_all | solution.py:130
  66.8 1.5 %shard_map.60 = (bf16[32,8,128]{2,1,0:T(8,128)(2,1)}, bf16[16,2,8,128]{3,2,1,0:T(8,128)(2,1)}) custom-call(f32[16,8,128]{2,1,0:T(8,128)} %all_to_all.21.tiles_ref), custom_call_target="tpu_custom_call" | custom-call | flops 16384 | bytes 196608 | tf_op jit(solution)/shard_map/pallas_call | solution.py:61
  68.3 20.1 %all_to_all.22 = bf16[32,8,128]{2,1,0:T(8,128)(2,1)S(1)} all-to-all(bf16[32,8,128]{2,1,0:T(8,128)(2,1)} %get-tuple-element.4), channel_id=1, replica_groups=mesh['row'=16,'col'=32] {'col'}, dimensions={0} | all-to-all | bytes 131072 | tf_op jit(solution)/shard_map/all_to_all | solution.py:131
  88.4 0.9 pad_maximum_fusion
  89.3 11.4 %all_to_all.23.refs_0_ = bf16[16,4,8,128]{3,2,1,0:T(8,128)(2,1)} all-to-all(bf16[16,4,8,128]{3,2,1,0:T(8,128)(2,1)S(1)} %pad_maximum_fusion), channel_id=1, replica_groups=mesh['row'=16,'col'=32] {'row'}, dimensions={0} | all-to-all | bytes 262144 | tf_op jit(solution)/shard_map/all_to_all | solution.py:133
  100.7 3.6 %shard_map.61 = (f32[64,256]{1,0:T(8,128)}, bf16[512,2048]{1,0:T(8,128)(2,1)}) custom-call(bf16[16,4,8,128]{3,2,1,0:T(8,128)(2,1)} %all_to_all.23.refs_0_, bf16[64,256]{1,0:T(8,128)(2,1)} %refs_1_.1, bf16[64,2048]{1,0:T(8,128)(2,1)} %refs_2_.1), custom_call_target="tpu_custom_call" | custom-call | flops 134217728 | bytes 2490368 | tf_op jit(solution)/shard_map/pallas_call | solution.py:105

commit v2 on v1

v2 whole, which is shorter than its diff:
```python
import jax
import jax.numpy as jnp
from jax import lax
from jax.experimental import pallas as pl
from jax.experimental.pallas import tpu as pltpu
from jax.sharding import Mesh, PartitionSpec as P

SUB, LANE = 8, 128
F32, BF16 = jnp.float32, jnp.bfloat16
COL = ("far", "near")
PARAMS = pltpu.CompilerParams(vmem_limit_bytes=8 << 20)


def full(shape):
    return pl.BlockSpec(shape, lambda *_: (0,) * len(shape))


def half_sum(parity, blocks_ref, slab_ref):
    pair = 2
    total = None
    for i in range(0, blocks_ref.shape[0], pair):
        left = jnp.concatenate([blocks_ref[i + j] for j in range(pair)], axis=1)
        right = jnp.concatenate([slab_ref[i + j, parity] for j in range(pair)], axis=0)
        term = jnp.dot(left, right, preferred_element_type=F32)
        total = term if total is None else total + term
    return total


def own_half_kernel(blocks_ref, slab_ref, out_ref):
    out_ref[...] = half_sum(lax.axis_index("near"), blocks_ref, slab_ref)


def other_half_kernel(blocks_ref, slab_ref, first_ref, out_ref):
    total = first_ref[...] + half_sum(1 - lax.axis_index("near"), blocks_ref, slab_ref)
    across = total.shape[1] // LANE
    for t in range(out_ref.shape[0]):
        i, j = t // across, t % across
        out_ref[t] = total[i * SUB : (i + 1) * SUB, j * LANE : (j + 1) * LANE]


def own_half(blocks, slab):
    n, k, b = blocks.shape
    width = slab.shape[-1]
    return pl.pallas_call(
        own_half_kernel,
        out_shape=jax.ShapeDtypeStruct((k, width), F32),
        compiler_params=PARAMS,
        cost_estimate=pl.CostEstimate(
            flops=2 * n * k * b * width, bytes_accessed=2 * blocks.size + slab.size, transcendentals=0
        ),
    )(blocks, slab)


def other_half(blocks, slab, first):
    n, k, b = blocks.shape
    width = slab.shape[-1]
    tiles = (k // SUB) * (width // LANE)
    return pl.pallas_call(
        other_half_kernel,
        out_shape=jax.ShapeDtypeStruct((tiles, SUB, LANE), F32),
        compiler_params=PARAMS,
        cost_estimate=pl.CostEstimate(
            flops=2 * n * k * b * width, bytes_accessed=2 * blocks.size + slab.size, transcendentals=0
        ),
    )(blocks, slab, first)


def reduced_kernel(tiles_ref, high_ref, own_ref):
    pulled = tiles_ref[0]
    for t in range(1, tiles_ref.shape[0]):
        pulled = pulled + tiles_ref[t]
    high = pulled.astype(BF16)
    low = (pulled - high.astype(F32)).astype(BF16)
    for t in range(high_ref.shape[0]):
        high_ref[t] = high
    for t in range(own_ref.shape[0]):
        own_ref[t, 0] = high
        own_ref[t, 1] = low


def reduced(tiles, copies):
    rows = tiles.shape[0]
    tile = tiles.shape[1:]
    return pl.pallas_call(
        reduced_kernel,
        out_shape=[jax.ShapeDtypeStruct((copies,) + tile, BF16), jax.ShapeDtypeStruct((rows, 2) + tile, BF16)],
        compiler_params=PARAMS,
        cost_estimate=pl.CostEstimate(flops=tiles.size, bytes_accessed=10 * tiles.size, transcendentals=0),
    )(tiles)


def product_kernel(scale, tiles_ref, direct_ref, panel_ref, factor_ref, out_ref, left_ref):
    rows, blocks = tiles_ref.shape[0], tiles_ref.shape[1] - 2
    across = direct_ref.shape[1] // LANE
    chunk = out_ref.shape[0]

    @pl.when(pl.program_id(0) == 0)
    def _():
        for t in range(rows):
            i, j = t // across, t % across
            at = slice(i * SUB, (i + 1) * SUB)
            for b in range(blocks):
                lane = (b * across + j) * LANE
                left_ref[lane // chunk, at, lane % chunk : lane % chunk + LANE] = tiles_ref[t, b].astype(F32)
            lanes = slice(j * LANE, (j + 1) * LANE)
            pulled = tiles_ref[t, blocks].astype(F32) + tiles_ref[t, blocks + 1].astype(F32)
            factor_ref[at, lanes] = (direct_ref[at, lanes].astype(F32) + pulled) * scale

    left = left_ref[pl.program_id(0)].astype(BF16)
    product = lax.dot_general(left, panel_ref[...], (((0,), (0,)), ((), ())), preferred_element_type=F32)
    out_ref[...] = (product * -scale).astype(BF16)


def products(tiles, direct, panel, scale):
    k, columns = panel.shape
    depth = (tiles.shape[1] - 2) * direct.shape[1]
    chunk = depth // 4

    def kernel(*refs):
        product_kernel(scale, *refs)

    return pl.pallas_call(
        kernel,
        grid=(depth // chunk,),
        in_specs=[full(tiles.shape), full(direct.shape), full(panel.shape)],
        out_specs=[full(direct.shape), pl.BlockSpec((chunk, columns), lambda i: (i, 0))],
        out_shape=[jax.ShapeDtypeStruct(direct.shape, F32), jax.ShapeDtypeStruct((depth, columns), BF16)],
        scratch_shapes=[pltpu.VMEM((depth // chunk, k, chunk), F32)],
        compiler_params=PARAMS,
        cost_estimate=pl.CostEstimate(
            flops=2 * k * depth * columns, bytes_accessed=2 * (depth * columns + panel.size), transcendentals=0
        ),
    )(tiles, direct, panel)


def exchange(x, axes):
    return lax.all_to_all(x, axes, 0, 0, tiled=True)


def body(inverse_slab, cot_solved, cot_direct, solved_panel):
    scale = 0.5 ** 0.5
    rows, far, near = (lax.axis_size(a) for a in ("row",) + COL)
    slab = inverse_slab.reshape(far, near, cot_solved.shape[1], inverse_slab.shape[1])
    mine = exchange(jnp.broadcast_to(cot_solved, (far,) + cot_solved.shape), "far")
    theirs = lax.ppermute(mine, "near", [(0, 1), (1, 0)])
    tiles = other_half(theirs, slab, own_half(mine, slab))
    high, own = reduced(exchange(tiles, "row"), far * near)
    every = exchange(high, COL).reshape((rows, far * near // rows) + high.shape[1:])
    needed = exchange(jnp.concatenate([every, own], axis=1), "row")
    return tuple(products(needed, cot_direct, solved_panel, scale))


def solution(mesh):
    near = 2
    rows, cols = mesh.devices.shape
    fine = Mesh(mesh.devices.reshape(rows, cols // near, near), ("row",) + COL)
    in_specs = (P("row", COL), P(None, ("row",) + COL), P(None, COL), P(None, COL))
    out_specs = (P(None, COL), P("row", COL))
    return jax.shard_map(body, mesh=fine, in_specs=in_specs, out_specs=out_specs, check_vma=False)
```

time: 105 us -> 95.5 us (0.910)
  blocking collectives: 94 us -> 82.1 us
  starting transfers between devices: 0 us -> 4.95 us
  Pallas kernels: 8.02 us -> 3.21 us
  waiting for transfers between devices: 0 us -> 1.82 us
  local copies, waits for them, and re-layouts: 0.83 us -> 2.36 us
    all_to_all x4, blocking collectives: 94 us -> 82.1 us  [exchange(): return lax.all_to_all(x, axes, 0, 0, tiled=True)]
    ppermute x0 -> x1, starting transfers between devices: none -> 4.95 us  [body(): theirs = lax.ppermute(mine, 'near', [(0, 1), (1, 0)])]
    pallas_call x1 -> x2, Pallas kernels: 2.88 us -> 0.6 us  [the longest x1 0.3 us: other_half(): pl.pallas_call(other_half_kernel, out_shape=jax.ShapeDtypeStruct((tiles,...]
    ppermute x0 -> x1, waiting for transfers between devices: none -> 1.82 us  [body(): theirs = lax.ppermute(mine, 'near', [(0, 1), (1, 0)])]
    unnamed x0 -> x8, local copies, waits for them, and re-layouts: none -> 1.6 us
    pallas_call x1, Pallas kernels: 1.51 us -> 0.03 us  [reduced(): pl.pallas_call(reduced_kernel, out_shape=[jax.ShapeDtypeStruct((copies,)...]
  transfers between devices with their start and end apart: 0 -> 1, of which waited for: 0 -> 1; matrix products, arithmetic and copies ran while one was open for 0% -> 0% of each run, Pallas kernels for 0% -> 0%
where the time goes in v2:
time: 95.5 us; the launch traced here: 95.1 us
  blocking collectives  82.1 us (86%)
  starting transfers between devices  4.95 us (5%)
  Pallas kernels  3.21 us (3%)
  local copies, waits for them, and re-layouts  2.36 us (2%)
  waiting for transfers between devices  1.82 us (2%)
    all_to_all x4, blocking collectives, exchange(): return lax.all_to_all(x, axes, 0, 0, tiled=True)  82.1 us
    ppermute x1, starting transfers between devices, body(): theirs = lax.ppermute(mine, 'near', [(0, 1), (1, 0)])  4.95 us
    pallas_call x1, Pallas kernels, products(): pl.pallas_call(kernel, grid=(depth // chunk,), in_specs=[full(tiles.shape...  2.59 us
  transfers between devices with their start and end apart: 1, of which 1 were waited for; matrix products, arithmetic and copies ran while one was open for 0% of the time, Pallas kernels for 0%

profile of v2, /device:TPU:1, one launch (start us, length us, event | category | flops | bytes accessed | tf_op | source)
XLA Modules:
  0.0 95.1 jit_solution(1096501669899413568)
XLA Ops:
  0.6 0.8 broadcast_in_dim.3
  1.4 32.4 %all_to_all.20.blocks_ref = bf16[16,64,128]{2,1,0:T(8,128)(2,1)S(1)} all-to-all(bf16[16,64,128]{2,1,0:T(8,128)(2,1)S(1)} %broadcast_in_dim.3), channel_id=1, replica_groups=mesh['row'=16,'far'=16,'near'=2] {'far'}, dimensions={0} | all-to-all | bytes 524288 | tf_op jit(solution)/shard_map/all_to_all | solution.py:137
  33.8 4.9 %collective-permute-start = (bf16[16,64,128]{2,1,0:T(8,128)(2,1)S(1)}, bf16[16,64,128]{2,1,0:T(8,128)(2,1)S(1)}, u32[]{:S(2)}, u32[]{:S(2)}) collective-permute-start(bf16[16,64,128]{2,1,0:T(8,128)(2,1)S(1)} %all_to_all.20.blocks_ref), channel_id=1, source_target_pairs={{0,1},{1,0},{2,3},{3,2},{4,5},{5,4},{6,7},{7,6},{8,9},{9,8},{10,11... | collective-permute-start | bytes 786440 | tf_op jit(solution)/shard_map/ppermute | solution.py:145
  38.8 0.0 copy-start
  38.8 1.6 %copy-done = bf16[4096,256]{1,0:T(8,128)(2,1)S(1)} copy-done((bf16[4096,256]{1,0:T(8,128)(2,1)S(1)}, bf16[4096,256]{1,0:T(8,128)(2,1)}, u32[]{:S(2)}) %copy-start) | copy-done | bytes 2097176
  40.4 0.0 copy-start.1
  40.4 0.3 shard_map.59.first_ref
  40.7 0.0 copy-start.2
  40.7 0.0 copy-start.3
  40.7 1.8 %collective-permute-done.blocks_ref = bf16[16,64,128]{2,1,0:T(8,128)(2,1)S(1)} collective-permute-done((bf16[16,64,128]{2,1,0:T(8,128)(2,1)S(1)}, bf16[16,64,128]{2,1,0:T(8,128)(2,1)S(1)}, u32[]{:S(2)}, u32[]{:S(2)}) %collective-permute-start) | collective-permute-done | bytes 262176 | tf_op jit(solution)/shard_map/ppermute | solution.py:145
  42.5 0.0 copy-done.1
  42.5 0.3 shard_map.60
  42.8 14.9 %all_to_all.21.tiles_ref = f32[16,8,128]{2,1,0:T(8,128)S(1)} all-to-all(f32[16,8,128]{2,1,0:T(8,128)S(1)} %shard_map.60), channel_id=1, replica_groups=mesh['row'=16,'far'=16,'near'=2] {'row'}, dimensions={0} | all-to-all | bytes 131072 | tf_op jit(solution)/shard_map/all_to_all | solution.py:137
  57.8 24.0 %all_to_all.22 = bf16[32,8,128]{2,1,0:T(8,128)(2,1)S(1)} all-to-all(bf16[32,8,128]{2,1,0:T(8,128)(2,1)S(1)} %get-tuple-element.4), channel_id=1, replica_groups=mesh['row'=16,'far'=16,'near'=2] {'far','near'}, dimensions={0} | all-to-all | bytes 131072 | tf_op jit(solution)/shard_map/all_to_all | solution.py:137
  81.7 10.8 %all_to_all.23.refs_0_ = bf16[16,4,8,128]{3,2,1,0:T(8,128)(2,1)S(1)} all-to-all(bf16[16,4,8,128]{3,2,1,0:T(8,128)(2,1)S(1)} %pad_maximum_fusion), channel_id=1, replica_groups=mesh['row'=16,'far'=16,'near'=2] {'row'}, dimensions={0} | all-to-all | bytes 262144 | tf_op jit(solution)/shard_map/all_to_all | solution.py:137
  92.5 0.0 copy-done.2
  92.5 0.0 copy-done.3
  92.5 2.6 %shard_map.62 = (f32[64,256]{1,0:T(8,128)}, bf16[512,2048]{1,0:T(8,128)(2,1)}) custom-call(bf16[16,4,8,128]{3,2,1,0:T(8,128)(2,1)S(1)} %all_to_all.23.refs_0_, bf16[64,256]{1,0:T(8,128)(2,1)S(1)} %copy-done.3, bf16[64,2048]{1,0:T(8,128)(2,1)S(1)} %copy-done.2), custom_call_target="tpu_custom_call" | custom-call | flops 134217728 | bytes 2359296 | tf_op jit(solution)/shard_map/pallas_call | solution.py:122
  (2 shorter events, 0.0 us)
Async XLA Ops:
  33.8 8.7 %collective-permute-start = (bf16[16,64,128]{2,1,0:T(8,128)(2,1)S(1)}, bf16[16,64,128]{2,1,0:T(8,128)(2,1)S(1)}, u32[]{:S(2)}, u32[]{:S(2)}) collective-permute-start(bf16[16,64,128]{2,1,0:T(8,128)(2,1)S(1)} %all_to_all.20.blocks_ref), channel_id=1, source_target_pairs={{0,1},{1,0},{2,3},{3,2},{4,5},{5,4},{6,7},{7,6},{8,9},{9,8},{10,11... | collective-permute-start | bytes 786440 | tf_op jit(solution)/shard_map/ppermute | solution.py:145
  38.8 1.6 %copy-start = (bf16[4096,256]{1,0:T(8,128)(2,1)S(1)}, bf16[4096,256]{1,0:T(8,128)(2,1)}, u32[]{:S(2)}) copy-start(bf16[4096,256]{1,0:T(8,128)(2,1)} %param.4) | copy-start | bytes 6291460
  40.4 2.2 %copy-start.1 = (bf16[4096,256]{1,0:T(8,128)(2,1)S(1)}, bf16[4096,256]{1,0:T(8,128)(2,1)}, u32[]{:S(2)}) copy-start(bf16[4096,256]{1,0:T(8,128)(2,1)} %param.4) | copy-start | bytes 6291460
  40.7 51.9 %copy-start.2 = (bf16[64,2048]{1,0:T(8,128)(2,1)S(1)}, bf16[64,2048]{1,0:T(8,128)(2,1)}, u32[]{:S(2)}) copy-start(bf16[64,2048]{1,0:T(8,128)(2,1)} %refs_2_.1) | copy-start | bytes 786436
  40.7 51.9 %copy-start.3 = (bf16[64,256]{1,0:T(8,128)(2,1)S(1)}, bf16[64,256]{1,0:T(8,128)(2,1)}, u32[]{:S(2)}) copy-start(bf16[64,256]{1,0:T(8,128)(2,1)} %refs_1_.1) | copy-start | bytes 98308

commit v3 on v2

--- a/solution.py
+++ b/solution.py
@@ -7,7 +7,8 @@
 
 SUB, LANE = 8, 128
 F32, BF16 = jnp.float32, jnp.bfloat16
-COL = ("far", "near")
+COL = ("half", "far", "near")
+CLOSE = ("half", "near")
 PARAMS = pltpu.CompilerParams(vmem_limit_bytes=8 << 20)
 
 
@@ -15,52 +16,59 @@
     return pl.BlockSpec(shape, lambda *_: (0,) * len(shape))
 
 
-def half_sum(parity, blocks_ref, slab_ref):
+def share_sum(half, near, blocks_ref, slab_ref, lead=()):
     pair = 2
     total = None
-    for i in range(0, blocks_ref.shape[0], pair):
-        left = jnp.concatenate([blocks_ref[i + j] for j in range(pair)], axis=1)
-        right = jnp.concatenate([slab_ref[i + j, parity] for j in range(pair)], axis=0)
+    for i in range(0, slab_ref.shape[1], pair):
+        left = jnp.concatenate([blocks_ref[lead + (i + j,)] for j in range(pair)], axis=1)
+        right = jnp.concatenate([slab_ref[half, i + j, near] for j in range(pair)], axis=0)
         term = jnp.dot(left, right, preferred_element_type=F32)
         total = term if total is None else total + term
     return total
 
 
-def own_half_kernel(blocks_ref, slab_ref, out_ref):
-    out_ref[...] = half_sum(lax.axis_index("near"), blocks_ref, slab_ref)
+def own_share_kernel(blocks_ref, slab_ref, out_ref):
+    out_ref[...] = share_sum(lax.axis_index("half"), lax.axis_index("near"), blocks_ref, slab_ref)
 
 
-def other_half_kernel(blocks_ref, slab_ref, first_ref, out_ref):
-    total = first_ref[...] + half_sum(1 - lax.axis_index("near"), blocks_ref, slab_ref)
+def other_shares_kernel(blocks_ref, slab_ref, first_ref, out_ref):
+    halves, _, nears = slab_ref.shape[:3]
+    half, near = lax.axis_index("half"), lax.axis_index("near")
+    total = first_ref[...]
+    for dh in range(halves):
+        for dn in range(nears):
+            if dh or dn:
+                h, n = lax.rem(half + dh, halves), lax.rem(near + dn, nears)
+                total = total + share_sum(h, n, blocks_ref, slab_ref, (h * nears + n,))
     across = total.shape[1] // LANE
     for t in range(out_ref.shape[0]):
         i, j = t // across, t % across
         out_ref[t] = total[i * SUB : (i + 1) * SUB, j * LANE : (j + 1) * LANE]
 
 
-def own_half(blocks, slab):
+def own_share(blocks, slab):
     n, k, b = blocks.shape
     width = slab.shape[-1]
     return pl.pallas_call(
-        own_half_kernel,
+        own_share_kernel,
         out_shape=jax.ShapeDtypeStruct((k, width), F32),
         compiler_params=PARAMS,
         cost_estimate=pl.CostEstimate(
-            flops=2 * n * k * b * width, bytes_accessed=2 * blocks.size + slab.size, transcendentals=0
+            flops=2 * n * k * b * width, bytes_accessed=2 * (blocks.size + n * b * width), transcendentals=0
         ),
     )(blocks, slab)
 
 
-def other_half(blocks, slab, first):
-    n, k, b = blocks.shape
+def other_shares(blocks, slab, first):
+    shares, n, k, b = blocks.shape
     width = slab.shape[-1]
     tiles = (k // SUB) * (width // LANE)
     return pl.pallas_call(
-        other_half_kernel,
+        other_shares_kernel,
         out_shape=jax.ShapeDtypeStruct((tiles, SUB, LANE), F32),
         compiler_params=PARAMS,
         cost_estimate=pl.CostEstimate(
-            flops=2 * n * k * b * width, bytes_accessed=2 * blocks.size + slab.size, transcendentals=0
+            flops=2 * shares * n * k * b * width, bytes_accessed=2 * (blocks.size + slab.size), transcendentals=0
         ),
     )(blocks, slab, first)
 
@@ -139,21 +147,22 @@
 
 def body(inverse_slab, cot_solved, cot_direct, solved_panel):
     scale = 0.5 ** 0.5
-    rows, far, near = (lax.axis_size(a) for a in ("row",) + COL)
-    slab = inverse_slab.reshape(far, near, cot_solved.shape[1], inverse_slab.shape[1])
+    rows, half, far, near = (lax.axis_size(a) for a in ("row",) + COL)
+    cols = half * far * near
+    slab = inverse_slab.reshape(half, far, near, cot_solved.shape[1], inverse_slab.shape[1])
     mine = exchange(jnp.broadcast_to(cot_solved, (far,) + cot_solved.shape), "far")
-    theirs = lax.ppermute(mine, "near", [(0, 1), (1, 0)])
-    tiles = other_half(theirs, slab, own_half(mine, slab))
-    high, own = reduced(exchange(tiles, "row"), far * near)
-    every = exchange(high, COL).reshape((rows, far * near // rows) + high.shape[1:])
+    shares = exchange(jnp.broadcast_to(mine, (half * near,) + mine.shape), CLOSE)
+    tiles = other_shares(shares, slab, own_share(mine, slab))
+    high, own = reduced(exchange(tiles, "row"), cols)
+    every = exchange(high, COL).reshape((rows, cols // rows) + high.shape[1:])
     needed = exchange(jnp.concatenate([every, own], axis=1), "row")
     return tuple(products(needed, cot_direct, solved_panel, scale))
 
 
 def solution(mesh):
-    near = 2
+    half, near = 2, 2
     rows, cols = mesh.devices.shape
-    fine = Mesh(mesh.devices.reshape(rows, cols // near, near), ("row",) + COL)
+    fine = Mesh(mesh.devices.reshape(rows, half, cols // (half * near), near), ("row",) + COL)
     in_specs = (P("row", COL), P(None, ("row",) + COL), P(None, COL), P(None, COL))
     out_specs = (P(None, COL), P("row", COL))
     return jax.shard_map(body, mesh=fine, in_specs=in_specs, out_specs=out_specs, check_vma=False)

time: 95.5 us -> 91.1 us (0.954)
  blocking collectives: 82.1 us -> 73.1 us
  waiting for transfers between devices: 1.82 us -> 6.69 us
    all_to_all x4, blocking collectives: 82.1 us -> 73.1 us  [exchange(): return lax.all_to_all(x, axes, 0, 0, tiled=True)]
    all_to_all x0 -> x1, waiting for transfers between devices: none -> 6.69 us  [exchange(): return lax.all_to_all(x, axes, 0, 0, tiled=True)]
    all_to_all x0 -> x1, starting transfers between devices: none -> 5.23 us  [exchange(): return lax.all_to_all(x, axes, 0, 0, tiled=True)]
    ppermute x1 -> x0, starting transfers between devices: 4.95 us -> none  [body(): theirs = lax.ppermute(mine, 'near', [(0, 1), (1, 0)])]
    ppermute x1 -> x0, waiting for transfers between devices: 1.82 us -> none  [body(): theirs = lax.ppermute(mine, 'near', [(0, 1), (1, 0)])]
    unnamed x8 -> x6, local copies, waits for them, and re-layouts: 1.6 us -> 0.02 us
where the time goes in v3:
time: 91.1 us; the launch traced here: 90.7 us
  blocking collectives  73.1 us (80%)
  waiting for transfers between devices  6.69 us (7%)
  starting transfers between devices  5.23 us (6%)
  Pallas kernels  3.21 us (4%)
  local copies, waits for them, and re-layouts  1.81 us (2%)
    all_to_all x4, blocking collectives, exchange(): return lax.all_to_all(x, axes, 0, 0, tiled=True)  73.1 us
    all_to_all x1, waiting for transfers between devices, exchange(): return lax.all_to_all(x, axes, 0, 0, tiled=True)  6.69 us
    all_to_all x1, starting transfers between devices, exchange(): return lax.all_to_all(x, axes, 0, 0, tiled=True)  5.23 us
    pallas_call x1, Pallas kernels, products(): pl.pallas_call(kernel, grid=(depth // chunk,), in_specs=[full(tiles.shape...  2.59 us
  transfers between devices with their start and end apart: 1, of which 1 were waited for; matrix products, arithmetic and copies ran while one was open for 0% of the time, Pallas kernels for 0%

profile of v3, /device:TPU:1, one launch (start us, length us, event | category | flops | bytes accessed | tf_op | source)
XLA Modules:
  0.0 90.7 jit_solution(7724871671099127549)
XLA Ops:
  0.6 0.0 copy-start
  0.6 0.9 broadcast_in_dim.6
  1.5 28.6 %all_to_all.25.blocks_ref = bf16[8,64,128]{2,1,0:T(8,128)(2,1)S(1)} all-to-all(bf16[8,64,128]{2,1,0:T(8,128)(2,1)S(1)} %broadcast_in_dim.6), channel_id=1, replica_groups=mesh['row'=16,'half'=2,'far'=8,'near'=2] {'far'}, dimensions={0} | all-to-all | bytes 262144 | tf_op jit(solution)/shard_map/all_to_all | solution.py:145
  30.1 0.9 %broadcast_in_dim.7 = bf16[4,8,64,128]{3,2,1,0:T(8,128)(2,1)} broadcast(bf16[8,64,128]{2,1,0:T(8,128)(2,1)S(1)} %all_to_all.25.blocks_ref), dimensions={1,2,3} | broadcast | bytes 655360 | tf_op jit(solution)/shard_map/broadcast_in_dim | solution.py:154
  31.0 5.2 %all-to-all-start.1 = ((bf16[4,8,64,128]{3,2,1,0:T(8,128)(2,1)}), bf16[4,8,64,128]{3,2,1,0:T(8,128)(2,1)S(1)}, u32[]{:S(2)}, u32[]{:S(2)}) async-start(bf16[4,8,64,128]{3,2,1,0:T(8,128)(2,1)} %broadcast_in_dim.7), calls=%async_computation.1 | async-start | bytes 1048576 | tf_op jit(solution)/shard_map/all_to_all | solution.py:145
  36.3 0.0 copy-done
  36.3 0.2 shard_map.59.first_ref
  36.5 0.0 copy-start.1
  36.5 0.0 copy-start.2
  36.5 6.7 %all-to-all-done.1.blocks_ref = bf16[4,8,64,128]{3,2,1,0:T(8,128)(2,1)S(1)} async-done(((bf16[4,8,64,128]{3,2,1,0:T(8,128)(2,1)}), bf16[4,8,64,128]{3,2,1,0:T(8,128)(2,1)S(1)}, u32[]{:S(2)}, u32[]{:S(2)}) %all-to-all-start.1) | async-done | bytes 524320 | tf_op jit(solution)/shard_map/all_to_all | solution.py:145
  43.2 0.4 shard_map.60
  43.6 14.4 %all_to_all.26.tiles_ref = f32[16,8,128]{2,1,0:T(8,128)S(1)} all-to-all(f32[16,8,128]{2,1,0:T(8,128)S(1)} %shard_map.60), channel_id=1, replica_groups=mesh['row'=16,'half'=2,'far'=8,'near'=2] {'row'}, dimensions={0} | all-to-all | bytes 131072 | tf_op jit(solution)/shard_map/all_to_all | solution.py:145
  58.0 19.4 %all_to_all.27 = bf16[32,8,128]{2,1,0:T(8,128)(2,1)S(1)} all-to-all(bf16[32,8,128]{2,1,0:T(8,128)(2,1)S(1)} %get-tuple-element.4), channel_id=1, replica_groups=mesh['row'=16,'half'=2,'far'=8,'near'=2] {'half','far','near'}, dimensions={0} | all-to-all | bytes 131072 | tf_op jit(solution)/shard_map/all_to_all | solution.py:145
  77.4 10.8 %all_to_all.28.refs_0_ = bf16[16,4,8,128]{3,2,1,0:T(8,128)(2,1)S(1)} all-to-all(bf16[16,4,8,128]{3,2,1,0:T(8,128)(2,1)S(1)} %pad_maximum_fusion), channel_id=1, replica_groups=mesh['row'=16,'half'=2,'far'=8,'near'=2] {'row'}, dimensions={0} | all-to-all | bytes 262144 | tf_op jit(solution)/shard_map/all_to_all | solution.py:145
  88.2 0.0 copy-done.1
  88.2 0.0 copy-done.2
  88.2 2.6 %shard_map.62 = (f32[64,256]{1,0:T(8,128)}, bf16[512,2048]{1,0:T(8,128)(2,1)}) custom-call(bf16[16,4,8,128]{3,2,1,0:T(8,128)(2,1)S(1)} %all_to_all.28.refs_0_, bf16[64,256]{1,0:T(8,128)(2,1)S(1)} %copy-done.2, bf16[64,2048]{1,0:T(8,128)(2,1)S(1)} %copy-done.1), custom_call_target="tpu_custom_call" | custom-call | flops 134217728 | bytes 2359296 | tf_op jit(solution)/shard_map/pallas_call | solution.py:130
  (2 shorter events, 0.0 us)
Async XLA Ops:
  0.6 35.6 %copy-start = (bf16[4096,256]{1,0:T(8,128)(2,1)S(1)}, bf16[4096,256]{1,0:T(8,128)(2,1)}, u32[]{:S(2)}) copy-start(bf16[4096,256]{1,0:T(8,128)(2,1)} %param.4) | copy-start | bytes 6291460
  31.0 12.2 %all-to-all-start.1 = ((bf16[4,8,64,128]{3,2,1,0:T(8,128)(2,1)}), bf16[4,8,64,128]{3,2,1,0:T(8,128)(2,1)S(1)}, u32[]{:S(2)}, u32[]{:S(2)}) async-start(bf16[4,8,64,128]{3,2,1,0:T(8,128)(2,1)} %broadcast_in_dim.7), calls=%async_computation.1 | async-start | bytes 1048576 | tf_op jit(solution)/shard_map/all_to_all | solution.py:145
  36.5 51.7 %copy-start.1 = (bf16[64,2048]{1,0:T(8,128)(2,1)S(1)}, bf16[64,2048]{1,0:T(8,128)(2,1)}, u32[]{:S(2)}) copy-start(bf16[64,2048]{1,0:T(8,128)(2,1)} %refs_2_.1) | copy-start | bytes 786436
  36.5 51.7 %copy-start.2 = (bf16[64,256]{1,0:T(8,128)(2,1)S(1)}, bf16[64,256]{1,0:T(8,128)(2,1)}, u32[]{:S(2)}) copy-start(bf16[64,256]{1,0:T(8,128)(2,1)} %refs_1_.1) | copy-start | bytes 98308

commit v4 on v3

--- a/solution.py
+++ b/solution.py
@@ -10,10 +10,6 @@
 COL = ("half", "far", "near")
 CLOSE = ("half", "near")
 PARAMS = pltpu.CompilerParams(vmem_limit_bytes=8 << 20)
-
-
-def full(shape):
-    return pl.BlockSpec(shape, lambda *_: (0,) * len(shape))
 
 
 def share_sum(half, near, blocks_ref, slab_ref, lead=()):
@@ -97,48 +93,71 @@
     )(tiles)
 
 
-def product_kernel(scale, tiles_ref, direct_ref, panel_ref, factor_ref, out_ref, left_ref):
+def product_kernel(scale, tiles_ref, direct_ref, panel_ref, factor_ref, out_ref, left_ref, sum_ref, wide_ref, sems):
     rows, blocks = tiles_ref.shape[0], tiles_ref.shape[1] - 2
     across = direct_ref.shape[1] // LANE
-    chunk = out_ref.shape[0]
-
-    @pl.when(pl.program_id(0) == 0)
-    def _():
-        for t in range(rows):
-            i, j = t // across, t % across
-            at = slice(i * SUB, (i + 1) * SUB)
-            for b in range(blocks):
-                lane = (b * across + j) * LANE
-                left_ref[lane // chunk, at, lane % chunk : lane % chunk + LANE] = tiles_ref[t, b].astype(F32)
-            lanes = slice(j * LANE, (j + 1) * LANE)
-            pulled = tiles_ref[t, blocks].astype(F32) + tiles_ref[t, blocks + 1].astype(F32)
-            factor_ref[at, lanes] = (direct_ref[at, lanes].astype(F32) + pulled) * scale
-
-    left = left_ref[pl.program_id(0)].astype(BF16)
-    product = lax.dot_general(left, panel_ref[...], (((0,), (0,)), ((), ())), preferred_element_type=F32)
-    out_ref[...] = (product * -scale).astype(BF16)
+    chunks = sems.shape[0] - 1
+    chunk = out_ref.shape[0] // chunks
+    for t in range(rows):
+        i, j = t // across, t % across
+        at = slice(i * SUB, (i + 1) * SUB)
+        for b in range(blocks):
+            lane = (b * across + j) * LANE
+            left_ref[at, lane : lane + LANE] = tiles_ref[t, b].astype(F32)
+        lanes = slice(j * LANE, (j + 1) * LANE)
+        pulled = tiles_ref[t, blocks].astype(F32) + tiles_ref[t, blocks + 1].astype(F32)
+        sum_ref[at, lanes] = (direct_ref[at, lanes].astype(F32) + pulled) * scale
+    copies = [pltpu.make_async_copy(sum_ref, factor_ref, sems.at[chunks])]
+    copies[0].start()
+    for c in range(chunks):
+        at = slice(c * chunk, (c + 1) * chunk)
+        left = left_ref[:, at].astype(BF16)
+        product = lax.dot_general(left, panel_ref[...], (((0,), (0,)), ((), ())), preferred_element_type=F32)
+        wide_ref[at] = (product * -scale).astype(BF16)
+        copies.append(pltpu.make_async_copy(wide_ref.at[at], out_ref.at[at], sems.at[c]))
+        copies[-1].start()
+    for copy in copies:
+        copy.wait()
 
 
 def products(tiles, direct, panel, scale):
     k, columns = panel.shape
     depth = (tiles.shape[1] - 2) * direct.shape[1]
-    chunk = depth // 4
+    chunks = 4
 
     def kernel(*refs):
         product_kernel(scale, *refs)
 
     return pl.pallas_call(
         kernel,
-        grid=(depth // chunk,),
-        in_specs=[full(tiles.shape), full(direct.shape), full(panel.shape)],
-        out_specs=[full(direct.shape), pl.BlockSpec((chunk, columns), lambda i: (i, 0))],
+        in_specs=[pl.BlockSpec(memory_space=pltpu.VMEM)] * 3,
+        out_specs=[pl.BlockSpec(memory_space=pl.ANY)] * 2,
         out_shape=[jax.ShapeDtypeStruct(direct.shape, F32), jax.ShapeDtypeStruct((depth, columns), BF16)],
-        scratch_shapes=[pltpu.VMEM((depth // chunk, k, chunk), F32)],
+        scratch_shapes=[
+            pltpu.VMEM((k, depth), F32),
+            pltpu.VMEM(direct.shape, F32),
+            pltpu.VMEM((depth, columns), BF16),
+            pltpu.SemaphoreType.DMA((chunks + 1,)),
+        ],
         compiler_params=PARAMS,
         cost_estimate=pl.CostEstimate(
             flops=2 * k * depth * columns, bytes_accessed=2 * (depth * columns + panel.size), transcendentals=0
         ),
     )(tiles, direct, panel)
+
+
+def copies_kernel(x_ref, out_ref):
+    for i in range(out_ref.shape[0]):
+        out_ref[i] = x_ref[...]
+
+
+def copies(x, n):
+    return pl.pallas_call(
+        copies_kernel,
+        out_shape=jax.ShapeDtypeStruct((n,) + x.shape, x.dtype),
+        compiler_params=PARAMS,
+        cost_estimate=pl.CostEstimate(flops=0, bytes_accessed=2 * (n + 1) * x.size, transcendentals=0),
+    )(x)
 
 
 def exchange(x, axes):
@@ -150,8 +169,8 @@
     rows, half, far, near = (lax.axis_size(a) for a in ("row",) + COL)
     cols = half * far * near
     slab = inverse_slab.reshape(half, far, near, cot_solved.shape[1], inverse_slab.shape[1])
-    mine = exchange(jnp.broadcast_to(cot_solved, (far,) + cot_solved.shape), "far")
-    shares = exchange(jnp.broadcast_to(mine, (half * near,) + mine.shape), CLOSE)
+    mine = exchange(copies(cot_solved, far), "far")
+    shares = exchange(copies(mine, half * near), CLOSE)
     tiles = other_shares(shares, slab, own_share(mine, slab))
     high, own = reduced(exchange(tiles, "row"), cols)
     every = exchange(high, COL).reshape((rows, cols // rows) + high.shape[1:])

time: 91.1 us -> 90.2 us (level)
  local copies, waits for them, and re-layouts: 1.81 us -> 0.88 us
    broadcast_in_dim x2 -> x0, local copies, waits for them, and re-layouts: 1.8 us -> none  [the longest x1 0.91 us: body(): jnp.broadcast_to(mine, (half * near,) + mine.shape)]
    pallas_call x1 -> x3, Pallas kernels: 2.59 us -> 2.56 us  [the longest x1 1.68 us: products(): pl.pallas_call(kernel, in_specs=[pl.BlockSpec(memory_space=pltpu.VMEM)] *...]
where the time goes in v4:
time: 90.2 us; the launch traced here: 89.8 us
  blocking collectives  73.1 us (81%)
  waiting for transfers between devices  6.69 us (7%)
  starting transfers between devices  5.23 us (6%)
  Pallas kernels  3.19 us (4%)
    all_to_all x4, blocking collectives, exchange(): return lax.all_to_all(x, axes, 0, 0, tiled=True)  73.1 us
    all_to_all x1, waiting for transfers between devices, exchange(): return lax.all_to_all(x, axes, 0, 0, tiled=True)  6.69 us
    all_to_all x1, starting transfers between devices, exchange(): return lax.all_to_all(x, axes, 0, 0, tiled=True)  5.23 us
  transfers between devices with their start and end apart: 1, of which 1 were waited for; matrix products, arithmetic and copies ran while one was open for 0% of the time, Pallas kernels for 0%

profile of v4, /device:TPU:1, one launch (start us, length us, event | category | flops | bytes accessed | tf_op | source)
XLA Modules:
  0.0 89.8 jit_solution(5486086625044195798)
XLA Ops:
  0.6 0.0 copy-start
  0.6 0.0 copy-start.1
  0.6 0.9 copy-done.1
  1.5 28.6 %all_to_all.25.x_ref.blocks_ref = bf16[8,64,128]{2,1,0:T(8,128)(2,1)S(1)} all-to-all(bf16[8,64,128]{2,1,0:T(8,128)(2,1)S(1)} %shard_map.59), channel_id=1, replica_groups=mesh['row'=16,'half'=2,'far'=8,'near'=2] {'far'}, dimensions={0} | all-to-all | bytes 262144 | tf_op jit(solution)/shard_map/all_to_all | solution.py:164
  30.1 0.9 shard_map.60
  31.0 5.2 %all-to-all-start.1 = ((bf16[4,8,64,128]{3,2,1,0:T(8,128)(2,1)}), bf16[4,8,64,128]{3,2,1,0:T(8,128)(2,1)S(1)}, u32[]{:S(2)}, u32[]{:S(2)}) async-start(bf16[4,8,64,128]{3,2,1,0:T(8,128)(2,1)} %shard_map.60), calls=%async_computation.1 | async-start | bytes 1048576 | tf_op jit(solution)/shard_map/all_to_all | solution.py:164
  36.2 0.0 copy-done
  36.2 0.2 shard_map.61.first_ref
  36.4 0.0 copy-start.2
  36.4 0.0 copy-start.3
  36.5 6.7 %all-to-all-done.1.blocks_ref = bf16[4,8,64,128]{3,2,1,0:T(8,128)(2,1)S(1)} async-done(((bf16[4,8,64,128]{3,2,1,0:T(8,128)(2,1)}), bf16[4,8,64,128]{3,2,1,0:T(8,128)(2,1)S(1)}, u32[]{:S(2)}, u32[]{:S(2)}) %all-to-all-start.1) | async-done | bytes 524320 | tf_op jit(solution)/shard_map/all_to_all | solution.py:164
  43.1 0.4 shard_map.62
  43.5 14.4 %all_to_all.26.tiles_ref = f32[16,8,128]{2,1,0:T(8,128)S(1)} all-to-all(f32[16,8,128]{2,1,0:T(8,128)S(1)} %shard_map.62), channel_id=1, replica_groups=mesh['row'=16,'half'=2,'far'=8,'near'=2] {'row'}, dimensions={0} | all-to-all | bytes 131072 | tf_op jit(solution)/shard_map/all_to_all | solution.py:164
  58.0 19.4 %all_to_all.27 = bf16[32,8,128]{2,1,0:T(8,128)(2,1)S(1)} all-to-all(bf16[32,8,128]{2,1,0:T(8,128)(2,1)S(1)} %get-tuple-element.4), channel_id=1, replica_groups=mesh['row'=16,'half'=2,'far'=8,'near'=2] {'half','far','near'}, dimensions={0} | all-to-all | bytes 131072 | tf_op jit(solution)/shard_map/all_to_all | solution.py:164
  77.3 10.8 %all_to_all.28.refs_0_ = bf16[16,4,8,128]{3,2,1,0:T(8,128)(2,1)S(1)} all-to-all(bf16[16,4,8,128]{3,2,1,0:T(8,128)(2,1)S(1)} %pad_maximum_fusion), channel_id=1, replica_groups=mesh['row'=16,'half'=2,'far'=8,'near'=2] {'row'}, dimensions={0} | all-to-all | bytes 262144 | tf_op jit(solution)/shard_map/all_to_all | solution.py:164
  88.1 0.0 copy-done.2
  88.1 0.0 copy-done.3
  88.1 1.7 %shard_map.64 = (f32[64,256]{1,0:T(8,128)}, bf16[512,2048]{1,0:T(8,128)(2,1)}) custom-call(bf16[16,4,8,128]{3,2,1,0:T(8,128)(2,1)S(1)} %all_to_all.28.refs_0_, bf16[64,256]{1,0:T(8,128)(2,1)S(1)} %copy-done.3, bf16[64,2048]{1,0:T(8,128)(2,1)S(1)} %copy-done.2), custom_call_target="tpu_custom_call" | custom-call | flops 134217728 | bytes 2359296 | tf_op jit(solution)/shard_map/pallas_call | solution.py:131
  (3 shorter events, 0.1 us)
Async XLA Ops:
  0.6 35.6 %copy-start = (bf16[4096,256]{1,0:T(8,128)(2,1)S(1)}, bf16[4096,256]{1,0:T(8,128)(2,1)}, u32[]{:S(2)}) copy-start(bf16[4096,256]{1,0:T(8,128)(2,1)} %param.4) | copy-start | bytes 6291460
  0.6 0.9 copy-start.1
  31.0 12.2 %all-to-all-start.1 = ((bf16[4,8,64,128]{3,2,1,0:T(8,128)(2,1)}), bf16[4,8,64,128]{3,2,1,0:T(8,128)(2,1)S(1)}, u32[]{:S(2)}, u32[]{:S(2)}) async-start(bf16[4,8,64,128]{3,2,1,0:T(8,128)(2,1)} %shard_map.60), calls=%async_computation.1 | async-start | bytes 1048576 | tf_op jit(solution)/shard_map/all_to_all | solution.py:164
  36.4 51.7 %copy-start.2 = (bf16[64,2048]{1,0:T(8,128)(2,1)S(1)}, bf16[64,2048]{1,0:T(8,128)(2,1)}, u32[]{:S(2)}) copy-start(bf16[64,2048]{1,0:T(8,128)(2,1)} %refs_2_.1) | copy-start | bytes 786436
  36.4 51.7 %copy-start.3 = (bf16[64,256]{1,0:T(8,128)(2,1)S(1)}, bf16[64,256]{1,0:T(8,128)(2,1)}, u32[]{:S(2)}) copy-start(bf16[64,256]{1,0:T(8,128)(2,1)} %refs_1_.1) | copy-start | bytes 98308

commit v5 on v4

--- a/solution.py
+++ b/solution.py
@@ -12,61 +12,33 @@
 PARAMS = pltpu.CompilerParams(vmem_limit_bytes=8 << 20)
 
 
-def share_sum(half, near, blocks_ref, slab_ref, lead=()):
-    pair = 2
+def partial_kernel(blocks_ref, slab_ref, out_ref):
+    halves, n, nears = slab_ref.shape[:3]
     total = None
-    for i in range(0, slab_ref.shape[1], pair):
-        left = jnp.concatenate([blocks_ref[lead + (i + j,)] for j in range(pair)], axis=1)
-        right = jnp.concatenate([slab_ref[half, i + j, near] for j in range(pair)], axis=0)
-        term = jnp.dot(left, right, preferred_element_type=F32)
-        total = term if total is None else total + term
-    return total
-
-
-def own_share_kernel(blocks_ref, slab_ref, out_ref):
-    out_ref[...] = share_sum(lax.axis_index("half"), lax.axis_index("near"), blocks_ref, slab_ref)
-
-
-def other_shares_kernel(blocks_ref, slab_ref, first_ref, out_ref):
-    halves, _, nears = slab_ref.shape[:3]
-    half, near = lax.axis_index("half"), lax.axis_index("near")
-    total = first_ref[...]
-    for dh in range(halves):
-        for dn in range(nears):
-            if dh or dn:
-                h, n = lax.rem(half + dh, halves), lax.rem(near + dn, nears)
-                total = total + share_sum(h, n, blocks_ref, slab_ref, (h * nears + n,))
+    for h in range(halves):
+        for i in range(n):
+            left = jnp.concatenate([blocks_ref[h * nears + m, i] for m in range(nears)], axis=1)
+            right = jnp.concatenate([slab_ref[h, i, m] for m in range(nears)], axis=0)
+            term = jnp.dot(left, right, preferred_element_type=F32)
+            total = term if total is None else total + term
     across = total.shape[1] // LANE
     for t in range(out_ref.shape[0]):
         i, j = t // across, t % across
         out_ref[t] = total[i * SUB : (i + 1) * SUB, j * LANE : (j + 1) * LANE]
 
 
-def own_share(blocks, slab):
-    n, k, b = blocks.shape
-    width = slab.shape[-1]
-    return pl.pallas_call(
-        own_share_kernel,
-        out_shape=jax.ShapeDtypeStruct((k, width), F32),
-        compiler_params=PARAMS,
-        cost_estimate=pl.CostEstimate(
-            flops=2 * n * k * b * width, bytes_accessed=2 * (blocks.size + n * b * width), transcendentals=0
-        ),
-    )(blocks, slab)
-
-
-def other_shares(blocks, slab, first):
+def partial_tiles(blocks, slab):
     shares, n, k, b = blocks.shape
     width = slab.shape[-1]
     tiles = (k // SUB) * (width // LANE)
     return pl.pallas_call(
-        other_shares_kernel,
+        partial_kernel,
         out_shape=jax.ShapeDtypeStruct((tiles, SUB, LANE), F32),
         compiler_params=PARAMS,
         cost_estimate=pl.CostEstimate(
             flops=2 * shares * n * k * b * width, bytes_accessed=2 * (blocks.size + slab.size), transcendentals=0
         ),
-    )(blocks, slab, first)
+    )(blocks, slab)
 
 
 def reduced_kernel(tiles_ref, high_ref, own_ref):
@@ -151,6 +123,26 @@
         out_ref[i] = x_ref[...]
 
 
+def fetched_copies_kernel(x_ref, out_ref, sems):
+    fetches = [pltpu.make_async_copy(x_ref, out_ref.at[i], sems.at[i]) for i in range(out_ref.shape[0])]
+    for fetch in fetches:
+        fetch.start()
+    for fetch in fetches:
+        fetch.wait()
+
+
+def fetched_copies(x, n):
+    return pl.pallas_call(
+        fetched_copies_kernel,
+        in_specs=[pl.BlockSpec(memory_space=pltpu.HBM)],
+        out_specs=pl.BlockSpec(memory_space=pltpu.VMEM),
+        out_shape=jax.ShapeDtypeStruct((n,) + x.shape, x.dtype),
+        scratch_shapes=[pltpu.SemaphoreType.DMA((n,))],
+        compiler_params=PARAMS,
+        cost_estimate=pl.CostEstimate(flops=0, bytes_accessed=4 * n * x.size, transcendentals=0),
+    )(x)
+
+
 def copies(x, n):
     return pl.pallas_call(
         copies_kernel,
@@ -169,9 +161,9 @@
     rows, half, far, near = (lax.axis_size(a) for a in ("row",) + COL)
     cols = half * far * near
     slab = inverse_slab.reshape(half, far, near, cot_solved.shape[1], inverse_slab.shape[1])
-    mine = exchange(copies(cot_solved, far), "far")
+    mine = exchange(fetched_copies(pltpu.with_memory_space_constraint(cot_solved, pltpu.HBM), far), "far")
     shares = exchange(copies(mine, half * near), CLOSE)
-    tiles = other_shares(shares, slab, own_share(mine, slab))
+    tiles = partial_tiles(shares, slab)
     high, own = reduced(exchange(tiles, "row"), cols)
     every = exchange(high, COL).reshape((rows, cols // rows) + high.shape[1:])
     needed = exchange(jnp.concatenate([every, own], axis=1), "row")

time: 90.2 us -> 89.5 us (level)
  blocking collectives: 73.1 us -> 85.2 us
  waiting for transfers between devices: 6.69 us -> 0 us
  starting transfers between devices: 5.23 us -> 0 us
    all_to_all x4 -> x5, blocking collectives: 73.1 us -> 85.2 us  [exchange(): return lax.all_to_all(x, axes, 0, 0, tiled=True)]
    all_to_all x1 -> x0, waiting for transfers between devices: 6.69 us -> none  [exchange(): return lax.all_to_all(x, axes, 0, 0, tiled=True)]
    all_to_all x1 -> x0, starting transfers between devices: 5.23 us -> none  [exchange(): return lax.all_to_all(x, axes, 0, 0, tiled=True)]
    pallas_call x2, Pallas kernels: 0.6 us -> 1.55 us  [the longest x1 1.08 us: fetched_copies(): pl.pallas_call(fetched_copies_kernel, in_specs=[pl.BlockSpec(memory_space...]
  transfers between devices with their start and end apart: 1 -> 0, of which waited for: 1 -> 0; matrix products, arithmetic and copies ran while one was open for 0% -> 0% of each run, Pallas kernels for 0% -> 0%
where the time goes in v5:
time: 89.5 us; the launch traced here: 89.2 us
  blocking collectives  85.2 us (95%)
  Pallas kernels  3.33 us (4%)
    all_to_all x5, blocking collectives, exchange(): return lax.all_to_all(x, axes, 0, 0, tiled=True)  85.2 us

profile of v5, /device:TPU:1, one launch (start us, length us, event | category | flops | bytes accessed | tf_op | source)
XLA Modules:
  0.0 89.2 jit_solution(15998423591278799198)
XLA Ops:
  0.6 0.0 copy-start
  0.6 1.1 %shard_map.59 = bf16[8,64,128]{2,1,0:T(8,128)(2,1)S(1)} custom-call(bf16[64,128]{1,0:T(8,128)(2,1)} %x_ref.1), custom_call_target="tpu_custom_call" | custom-call | bytes 262144 | tf_op jit(solution)/shard_map/pallas_call | solution.py:135
  1.7 28.6 %all_to_all.25.x_ref = bf16[8,64,128]{2,1,0:T(8,128)(2,1)S(1)} all-to-all(bf16[8,64,128]{2,1,0:T(8,128)(2,1)S(1)} %shard_map.59), channel_id=1, replica_groups=mesh['row'=16,'half'=2,'far'=8,'near'=2] {'far'}, dimensions={0} | all-to-all | bytes 262144 | tf_op jit(solution)/shard_map/all_to_all | solution.py:156
  30.3 0.1 shard_map.60
  30.4 0.0 copy-start.1
  30.4 0.0 copy-start.2
  30.4 12.6 %all_to_all.26.blocks_ref = bf16[4,8,64,128]{3,2,1,0:T(8,128)(2,1)S(1)} all-to-all(bf16[4,8,64,128]{3,2,1,0:T(8,128)(2,1)S(1)} %shard_map.60), channel_id=1, replica_groups=mesh['row'=16,'half'=2,'far'=8,'near'=2] {'half','near'}, dimensions={0} | all-to-all | bytes 1048576 | tf_op jit(solution)/shard_map/all_to_all | solution.py:156
  43.1 0.0 copy-done
  43.1 0.5 shard_map.61
  43.5 14.4 %all_to_all.27.tiles_ref = f32[16,8,128]{2,1,0:T(8,128)S(1)} all-to-all(f32[16,8,128]{2,1,0:T(8,128)S(1)} %shard_map.61), channel_id=1, replica_groups=mesh['row'=16,'half'=2,'far'=8,'near'=2] {'row'}, dimensions={0} | all-to-all | bytes 131072 | tf_op jit(solution)/shard_map/all_to_all | solution.py:156
  58.0 18.8 %all_to_all.28 = bf16[32,8,128]{2,1,0:T(8,128)(2,1)S(1)} all-to-all(bf16[32,8,128]{2,1,0:T(8,128)(2,1)S(1)} %get-tuple-element.4), channel_id=1, replica_groups=mesh['row'=16,'half'=2,'far'=8,'near'=2] {'half','far','near'}, dimensions={0} | all-to-all | bytes 131072 | tf_op jit(solution)/shard_map/all_to_all | solution.py:156
  76.7 10.8 %all_to_all.29.refs_0_ = bf16[16,4,8,128]{3,2,1,0:T(8,128)(2,1)S(1)} all-to-all(bf16[16,4,8,128]{3,2,1,0:T(8,128)(2,1)S(1)} %pad_maximum_fusion), channel_id=1, replica_groups=mesh['row'=16,'half'=2,'far'=8,'near'=2] {'row'}, dimensions={0} | all-to-all | bytes 262144 | tf_op jit(solution)/shard_map/all_to_all | solution.py:156
  87.5 0.0 copy-done.1
  87.5 0.0 copy-done.2
  87.5 1.7 %shard_map.63 = (f32[64,256]{1,0:T(8,128)}, bf16[512,2048]{1,0:T(8,128)(2,1)}) custom-call(bf16[16,4,8,128]{3,2,1,0:T(8,128)(2,1)S(1)} %all_to_all.29.refs_0_, bf16[64,256]{1,0:T(8,128)(2,1)S(1)} %copy-done.2, bf16[64,2048]{1,0:T(8,128)(2,1)S(1)} %copy-done.1), custom_call_target="tpu_custom_call" | custom-call | flops 134217728 | bytes 2359296 | tf_op jit(solution)/shard_map/pallas_call | solution.py:103
  (2 shorter events, 0.0 us)
Async XLA Ops:
  0.6 42.4 %copy-start = (bf16[4096,256]{1,0:T(8,128)(2,1)S(1)}, bf16[4096,256]{1,0:T(8,128)(2,1)}, u32[]{:S(2)}) copy-start(bf16[4096,256]{1,0:T(8,128)(2,1)} %param.4) | copy-start | bytes 6291460
  30.4 57.1 %copy-start.1 = (bf16[64,2048]{1,0:T(8,128)(2,1)S(1)}, bf16[64,2048]{1,0:T(8,128)(2,1)}, u32[]{:S(2)}) copy-start(bf16[64,2048]{1,0:T(8,128)(2,1)} %refs_2_.1) | copy-start | bytes 786436
  30.4 57.1 %copy-start.2 = (bf16[64,256]{1,0:T(8,128)(2,1)S(1)}, bf16[64,256]{1,0:T(8,128)(2,1)}, u32[]{:S(2)}) copy-start(bf16[64,256]{1,0:T(8,128)(2,1)} %refs_1_.1) | copy-start | bytes 98308

commit v6 on v5

--- a/solution.py
+++ b/solution.py
@@ -1,5 +1,8 @@
+import math
+
 import jax
 import jax.numpy as jnp
+import numpy as np
 from jax import lax
 from jax.experimental import pallas as pl
 from jax.experimental.pallas import tpu as pltpu
@@ -7,8 +10,10 @@
 
 SUB, LANE = 8, 128
 F32, BF16 = jnp.float32, jnp.bfloat16
-COL = ("half", "far", "near")
+FAR = ("z3", "z2", "z1")
+COL = ("half",) + FAR + ("near",)
 CLOSE = ("half", "near")
+SPREAD = ("near", "z1", "z2", "z3", "half")
 PARAMS = pltpu.CompilerParams(vmem_limit_bytes=8 << 20)
 
 
@@ -123,12 +128,12 @@
         out_ref[i] = x_ref[...]
 
 
-def fetched_copies_kernel(x_ref, out_ref, sems):
-    fetches = [pltpu.make_async_copy(x_ref, out_ref.at[i], sems.at[i]) for i in range(out_ref.shape[0])]
-    for fetch in fetches:
-        fetch.start()
-    for fetch in fetches:
-        fetch.wait()
+def fetched_copies_kernel(x_ref, out_ref, sem):
+    fetch = pltpu.make_async_copy(x_ref, out_ref.at[0], sem)
+    fetch.start()
+    fetch.wait()
+    for i in range(1, out_ref.shape[0]):
+        out_ref[i] = out_ref[0]
 
 
 def fetched_copies(x, n):
@@ -137,10 +142,34 @@
         in_specs=[pl.BlockSpec(memory_space=pltpu.HBM)],
         out_specs=pl.BlockSpec(memory_space=pltpu.VMEM),
         out_shape=jax.ShapeDtypeStruct((n,) + x.shape, x.dtype),
-        scratch_shapes=[pltpu.SemaphoreType.DMA((n,))],
+        scratch_shapes=[pltpu.SemaphoreType.DMA],
         compiler_params=PARAMS,
         cost_estimate=pl.CostEstimate(flops=0, bytes_accessed=4 * n * x.size, transcendentals=0),
-    )(x)
+    )(pltpu.with_memory_space_constraint(x, pltpu.HBM))
+
+
+def joined_kernel(order, every_ref, own_ref, out_ref):
+    rows, blocks = out_ref.shape[0], out_ref.shape[1] - own_ref.shape[1]
+    for t in range(rows):
+        for b in range(blocks):
+            out_ref[t, b] = every_ref[order[t * blocks + b]]
+        out_ref[t, blocks:] = own_ref[t]
+
+
+def joined(order, every, own):
+    rows = own.shape[0]
+    blocks = every.shape[0] // rows
+
+    def kernel(*refs):
+        joined_kernel(order, *refs)
+
+    shape = (rows, blocks + own.shape[1]) + own.shape[2:]
+    return pl.pallas_call(
+        kernel,
+        out_shape=jax.ShapeDtypeStruct(shape, own.dtype),
+        compiler_params=PARAMS,
+        cost_estimate=pl.CostEstimate(flops=0, bytes_accessed=4 * (every.size + own.size), transcendentals=0),
+    )(every, own)
 
 
 def copies(x, n):
@@ -156,24 +185,28 @@
     return lax.all_to_all(x, axes, 0, 0, tiled=True)
 
 
+def places(sizes):
+    grid = np.arange(math.prod(sizes.values())).reshape([sizes[a] for a in SPREAD])
+    return grid.transpose([SPREAD.index(a) for a in COL]).reshape(-1).tolist()
+
+
 def body(inverse_slab, cot_solved, cot_direct, solved_panel):
     scale = 0.5 ** 0.5
-    rows, half, far, near = (lax.axis_size(a) for a in ("row",) + COL)
-    cols = half * far * near
+    sizes = {a: lax.axis_size(a) for a in COL}
+    half, near = sizes["half"], sizes["near"]
+    far = math.prod(sizes[a] for a in FAR)
     slab = inverse_slab.reshape(half, far, near, cot_solved.shape[1], inverse_slab.shape[1])
-    mine = exchange(fetched_copies(pltpu.with_memory_space_constraint(cot_solved, pltpu.HBM), far), "far")
-    shares = exchange(copies(mine, half * near), CLOSE)
+    first = fetched_copies(cot_solved, far)
+    shares = exchange(copies(exchange(first, FAR), half * near), CLOSE)
     tiles = partial_tiles(shares, slab)
-    high, own = reduced(exchange(tiles, "row"), cols)
-    every = exchange(high, COL).reshape((rows, cols // rows) + high.shape[1:])
-    needed = exchange(jnp.concatenate([every, own], axis=1), "row")
+    high, own = reduced(exchange(tiles, "row"), half * far * near)
+    needed = exchange(joined(places(sizes), exchange(high, SPREAD), own), "row")
     return tuple(products(needed, cot_direct, solved_panel, scale))
 
 
 def solution(mesh):
-    half, near = 2, 2
     rows, cols = mesh.devices.shape
-    fine = Mesh(mesh.devices.reshape(rows, half, cols // (half * near), near), ("row",) + COL)
+    fine = Mesh(mesh.devices.reshape(rows, 2, cols // 16, 2, 2, 2), ("row",) + COL)
     in_specs = (P("row", COL), P(None, ("row",) + COL), P(None, COL), P(None, COL))
     out_specs = (P(None, COL), P("row", COL))
     return jax.shard_map(body, mesh=fine, in_specs=in_specs, out_specs=out_specs, check_vma=False)

time: 89.5 us -> 88.1 us (0.984)
  blocking collectives: 85.2 us -> 83.9 us
    all_to_all x5, blocking collectives: 85.2 us -> 83.9 us  [exchange(): return lax.all_to_all(x, axes, 0, 0, tiled=True)]
where the time goes in v6:
time: 88.1 us; the launch traced here: 87.8 us
  blocking collectives  83.9 us (95%)
  Pallas kernels  3.17 us (4%)
    all_to_all x5, blocking collectives, exchange(): return lax.all_to_all(x, axes, 0, 0, tiled=True)  83.9 us

profile of v6, /device:TPU:1, one launch (start us, length us, event | category | flops | bytes accessed | tf_op | source)
XLA Modules:
  0.0 87.8 jit_solution(8033762010652682202)
XLA Ops:
  0.6 0.0 copy-start
  0.6 0.9 %shard_map.59 = bf16[8,64,128]{2,1,0:T(8,128)(2,1)S(1)} custom-call(bf16[64,128]{1,0:T(8,128)(2,1)} %x_ref.1), custom_call_target="tpu_custom_call" | custom-call | bytes 262144 | tf_op jit(solution)/shard_map/pallas_call | solution.py:140
  1.5 28.6 %all_to_all.25.x_ref = bf16[8,64,128]{2,1,0:T(8,128)(2,1)S(1)} all-to-all(bf16[8,64,128]{2,1,0:T(8,128)(2,1)S(1)} %shard_map.59), channel_id=1, replica_groups=mesh['row'=16,'half'=2,'z3'=2,'z2'=2,'z1'=2,'near'=2] {'z3','z2','z1'}, dimensions={0} | all-to-all | bytes 262144 | tf_op jit(solution)/shard_map/all_to_all | solution.py:185
  30.1 0.1 shard_map.60
  30.2 0.0 copy-start.1
  30.2 0.0 copy-start.2
  30.2 12.6 %all_to_all.26.blocks_ref = bf16[4,8,64,128]{3,2,1,0:T(8,128)(2,1)S(1)} all-to-all(bf16[4,8,64,128]{3,2,1,0:T(8,128)(2,1)S(1)} %shard_map.60), channel_id=1, replica_groups=mesh['row'=16,'half'=2,'z3'=2,'z2'=2,'z1'=2,'near'=2] {'half','near'}, dimensions={0} | all-to-all | bytes 1048576 | tf_op jit(solution)/shard_map/all_to_all | solution.py:185
  42.9 0.0 copy-done
  42.9 0.5 shard_map.61
  43.4 14.4 %all_to_all.27.tiles_ref = f32[16,8,128]{2,1,0:T(8,128)S(1)} all-to-all(f32[16,8,128]{2,1,0:T(8,128)S(1)} %shard_map.61), channel_id=1, replica_groups=mesh['row'=16,'half'=2,'z3'=2,'z2'=2,'z1'=2,'near'=2] {'row'}, dimensions={0} | all-to-all | bytes 131072 | tf_op jit(solution)/shard_map/all_to_all | solution.py:185
  57.8 17.6 %all_to_all.28.refs_0_ = bf16[32,8,128]{2,1,0:T(8,128)(2,1)S(1)} all-to-all(bf16[32,8,128]{2,1,0:T(8,128)(2,1)S(1)} %get-tuple-element.4), channel_id=1, replica_groups=mesh['row'=16,'half'=2,'z3'=2,'z2'=2,'z1'=2,'near'=2] {'near','z1','z2',..., dimensions={0} | all-to-all | bytes 131072 | tf_op jit(solution)/shard_map/all_to_all | solution.py:185
  75.4 10.7 %all_to_all.29.refs_0_ = bf16[16,4,8,128]{3,2,1,0:T(8,128)(2,1)S(1)} all-to-all(bf16[16,4,8,128]{3,2,1,0:T(8,128)(2,1)S(1)} %shard_map.63), channel_id=1, replica_groups=mesh['row'=16,'half'=2,'z3'=2,'z2'=2,'z1'=2,'near'=2] {'row'}, dimensions={0} | all-to-all | bytes 262144 | tf_op jit(solution)/shard_map/all_to_all | solution.py:185
  86.1 0.0 copy-done.1
  86.1 0.0 copy-done.2
  86.1 1.7 %shard_map.64 = (f32[64,256]{1,0:T(8,128)}, bf16[512,2048]{1,0:T(8,128)(2,1)}) custom-call(bf16[16,4,8,128]{3,2,1,0:T(8,128)(2,1)S(1)} %all_to_all.29.refs_0_, bf16[64,256]{1,0:T(8,128)(2,1)S(1)} %copy-done.2, bf16[64,2048]{1,0:T(8,128)(2,1)S(1)} %copy-done.1), custom_call_target="tpu_custom_call" | custom-call | flops 134217728 | bytes 2359296 | tf_op jit(solution)/shard_map/pallas_call | solution.py:108
  (2 shorter events, 0.0 us)
Async XLA Ops:
  0.6 42.2 %copy-start = (bf16[4096,256]{1,0:T(8,128)(2,1)S(1)}, bf16[4096,256]{1,0:T(8,128)(2,1)}, u32[]{:S(2)}) copy-start(bf16[4096,256]{1,0:T(8,128)(2,1)} %param.4) | copy-start | bytes 6291460
  30.2 55.9 %copy-start.1 = (bf16[64,2048]{1,0:T(8,128)(2,1)S(1)}, bf16[64,2048]{1,0:T(8,128)(2,1)}, u32[]{:S(2)}) copy-start(bf16[64,2048]{1,0:T(8,128)(2,1)} %refs_2_.1) | copy-start | bytes 786436
  30.2 55.9 %copy-start.2 = (bf16[64,256]{1,0:T(8,128)(2,1)S(1)}, bf16[64,256]{1,0:T(8,128)(2,1)}, u32[]{:S(2)}) copy-start(bf16[64,256]{1,0:T(8,128)(2,1)} %refs_1_.1) | copy-start | bytes 98308

commit v7 on v6

--- a/solution.py
+++ b/solution.py
@@ -1,43 +1,41 @@
-import math
-
 import jax
 import jax.numpy as jnp
-import numpy as np
 from jax import lax
 from jax.experimental import pallas as pl
 from jax.experimental.pallas import tpu as pltpu
-from jax.sharding import Mesh, PartitionSpec as P
+from jax.sharding import PartitionSpec as P
 
 SUB, LANE = 8, 128
 F32, BF16 = jnp.float32, jnp.bfloat16
-FAR = ("z3", "z2", "z1")
-COL = ("half",) + FAR + ("near",)
-CLOSE = ("half", "near")
-SPREAD = ("near", "z1", "z2", "z3", "half")
+ROW_FIRST, COL_FIRST = 12, 26
 PARAMS = pltpu.CompilerParams(vmem_limit_bytes=8 << 20)
 
 
-def partial_kernel(blocks_ref, slab_ref, out_ref):
-    halves, n, nears = slab_ref.shape[:3]
+def partial_kernel(order, blocks_ref, slab_ref, out_ref):
+    where = {c: (q, i) for q, row in enumerate(order) for i, c in enumerate(row)}
+    pair = 2
     total = None
-    for h in range(halves):
-        for i in range(n):
-            left = jnp.concatenate([blocks_ref[h * nears + m, i] for m in range(nears)], axis=1)
-            right = jnp.concatenate([slab_ref[h, i, m] for m in range(nears)], axis=0)
-            term = jnp.dot(left, right, preferred_element_type=F32)
-            total = term if total is None else total + term
+    for c in range(0, slab_ref.shape[0], pair):
+        left = jnp.concatenate([blocks_ref[where[c + m]] for m in range(pair)], axis=1)
+        right = jnp.concatenate([slab_ref[c + m] for m in range(pair)], axis=0)
+        term = jnp.dot(left, right, preferred_element_type=F32)
+        total = term if total is None else total + term
     across = total.shape[1] // LANE
     for t in range(out_ref.shape[0]):
         i, j = t // across, t % across
         out_ref[t] = total[i * SUB : (i + 1) * SUB, j * LANE : (j + 1) * LANE]
 
 
-def partial_tiles(blocks, slab):
+def partial_tiles(order, blocks, slab):
     shares, n, k, b = blocks.shape
     width = slab.shape[-1]
     tiles = (k // SUB) * (width // LANE)
-    return pl.pallas_call(
-        partial_kernel,
+
+    def kernel(*refs):
+        partial_kernel(order, *refs)
+
+    return pl.pallas_call(
+        kernel,
         out_shape=jax.ShapeDtypeStruct((tiles, SUB, LANE), F32),
         compiler_params=PARAMS,
         cost_estimate=pl.CostEstimate(
@@ -181,32 +179,42 @@
     )(x)
 
 
-def exchange(x, axes):
-    return lax.all_to_all(x, axes, 0, 0, tiled=True)
-
-
-def places(sizes):
-    grid = np.arange(math.prod(sizes.values())).reshape([sizes[a] for a in SPREAD])
-    return grid.transpose([SPREAD.index(a) for a in COL]).reshape(-1).tolist()
+def reversed_bits(i, bits):
+    return sum(((i >> b) & 1) << (bits - 1 - b) for b in range(bits))
+
+
+def exchange(x, axis, groups):
+    return lax.all_to_all(x, axis, 0, 0, tiled=True, axis_index_groups=groups)
 
 
 def body(inverse_slab, cot_solved, cot_direct, solved_panel):
     scale = 0.5 ** 0.5
-    sizes = {a: lax.axis_size(a) for a in COL}
-    half, near = sizes["half"], sizes["near"]
-    far = math.prod(sizes[a] for a in FAR)
-    slab = inverse_slab.reshape(half, far, near, cot_solved.shape[1], inverse_slab.shape[1])
-    first = fetched_copies(cot_solved, far)
-    shares = exchange(copies(exchange(first, FAR), half * near), CLOSE)
-    tiles = partial_tiles(shares, slab)
-    high, own = reduced(exchange(tiles, "row"), half * far * near)
-    needed = exchange(joined(places(sizes), exchange(high, SPREAD), own), "row")
-    return tuple(products(needed, cot_direct, solved_panel, scale))
+    rows, cols = lax.axis_size("row"), lax.axis_size("col")
+    halves, nears = 2, 2
+    fars = cols // (halves * nears)
+    half0, far0, near0 = COL_FIRST // (fars * nears), COL_FIRST // nears % fars, COL_FIRST % nears
+
+    def col(half, far, near):
+        return ((half ^ half0) * fars + (far ^ far0)) * nears + (near ^ near0)
+
+    close = [(h, m) for h in range(halves) for m in range(nears)]
+    far_groups = [[col(h, f, m) for f in range(fars)] for h, m in close]
+    close_groups = [[col(h, f, m) for h, m in close] for f in range(fars)]
+    every_col = [COL_FIRST ^ reversed_bits(i, cols.bit_length() - 1) for i in range(cols)]
+    every_row = [ROW_FIRST ^ i for i in range(rows)]
+
+    slab = inverse_slab.reshape(cols, cot_solved.shape[1], inverse_slab.shape[1])
+    shares = copies(exchange(fetched_copies(cot_solved, fars), "col", far_groups), halves * nears)
+    shares = exchange(shares, "col", close_groups)
+    tiles = partial_tiles(far_groups, shares, slab)
+    high, own = reduced(exchange(tiles, "row", [every_row]), cols)
+    every = exchange(high, "col", [every_col])
+    needed = [every_col.index(r * (cols // rows) + b) for r in every_row for b in range(cols // rows)]
+    tiles = exchange(joined(needed, every, own), "row", [every_row])
+    return tuple(products(tiles, cot_direct, solved_panel, scale))
 
 
 def solution(mesh):
-    rows, cols = mesh.devices.shape
-    fine = Mesh(mesh.devices.reshape(rows, 2, cols // 16, 2, 2, 2), ("row",) + COL)
-    in_specs = (P("row", COL), P(None, ("row",) + COL), P(None, COL), P(None, COL))
-    out_specs = (P(None, COL), P("row", COL))
-    return jax.shard_map(body, mesh=fine, in_specs=in_specs, out_specs=out_specs, check_vma=False)
+    in_specs = (P("row", "col"), P(None, ("row", "col")), P(None, "col"), P(None, "col"))
+    out_specs = (P(None, "col"), P("row", "col"))
+    return jax.shard_map(body, mesh=mesh, in_specs=in_specs, out_specs=out_specs, check_vma=False)

time: 88.1 us -> 78.8 us (0.89)
  blocking collectives: 83.9 us -> 74.6 us
    all_to_all x5, blocking collectives: 83.9 us -> 74.6 us  [exchange(): return lax.all_to_all(x, axis, 0, 0, tiled=True, axis_index_groups=groups)]
where the time goes in v7:
time: 78.8 us; the launch traced here: 78.4 us
  blocking collectives  74.6 us (95%)
  Pallas kernels  3.17 us (4%)
    all_to_all x5, blocking collectives, exchange(): return lax.all_to_all(x, axis, 0, 0, tiled=True, axis_index_groups=groups)  74.6 us
    pallas_call x1, Pallas kernels, products(): pl.pallas_call(kernel, in_specs=[pl.BlockSpec(memory_space=pltpu.VMEM)] *...  1.69 us

profile of v7, /device:TPU:1, one launch (start us, length us, event | category | flops | bytes accessed | tf_op | source)
XLA Modules:
  0.0 78.4 jit_solution(4723822408440126244)
XLA Ops:
  0.6 0.0 copy-start
  0.6 0.9 %shard_map.59 = bf16[8,64,128]{2,1,0:T(8,128)(2,1)S(1)} custom-call(bf16[64,128]{1,0:T(8,128)(2,1)} %x_ref.1), custom_call_target="tpu_custom_call" | custom-call | bytes 262144 | tf_op jit(solution)/shard_map/pallas_call | solution.py:138
  1.5 24.7 %all_to_all.25.x_ref = bf16[8,64,128]{2,1,0:T(8,128)(2,1)S(1)} all-to-all(bf16[8,64,128]{2,1,0:T(8,128)(2,1)S(1)} %shard_map.59), channel_id=1, replica_groups={{26,24,30,28,18,16,22,20},{27,25,31,29,19,17,23,21},{10,8,14,12,2,0,6,4..., dimensions={0} | all-to-all | bytes 262144 | tf_op jit(solution)/shard_map/all_to_all | solution.py:187
  26.2 0.1 shard_map.60
  26.3 0.0 copy-start.1
  26.3 0.0 copy-start.2
  26.3 11.6 %all_to_all.26.refs_0_ = bf16[4,8,64,128]{3,2,1,0:T(8,128)(2,1)S(1)} all-to-all(bf16[4,8,64,128]{3,2,1,0:T(8,128)(2,1)S(1)} %shard_map.60), channel_id=1, replica_groups={{26,27,10,11},{24,25,8,9},{30,31,14,15},{28,29,12,13},{18,19,2,3},{16,1..., dimensions={0} | all-to-all | bytes 1048576 | tf_op jit(solution)/shard_map/all_to_all | solution.py:187
  37.9 0.0 copy-done
  37.9 0.5 shard_map.61
  38.4 10.9 %all_to_all.27.tiles_ref = f32[16,8,128]{2,1,0:T(8,128)S(1)} all-to-all(f32[16,8,128]{2,1,0:T(8,128)S(1)} %shard_map.61), channel_id=1, replica_groups={{384,416,448,480,256,288,320,352,128,160,192,224,0,32,64,96},{385,417,4..., dimensions={0} | all-to-all | bytes 131072 | tf_op jit(solution)/shard_map/all_to_all | solution.py:187
  49.3 17.2 %all_to_all.28.refs_0_ = bf16[32,8,128]{2,1,0:T(8,128)(2,1)S(1)} all-to-all(bf16[32,8,128]{2,1,0:T(8,128)(2,1)S(1)} %get-tuple-element.4), channel_id=1, replica_groups={{26,10,18,2,30,14,22,6,24,8,16,0,28,12,20,4,27,11,19,3,31,15,23,7,25,9,..., dimensions={0} | all-to-all | bytes 131072 | tf_op jit(solution)/shard_map/all_to_all | solution.py:187
  66.6 10.1 %all_to_all.29.refs_0_ = bf16[16,4,8,128]{3,2,1,0:T(8,128)(2,1)S(1)} all-to-all(bf16[16,4,8,128]{3,2,1,0:T(8,128)(2,1)S(1)} %shard_map.63), channel_id=1, replica_groups={{384,416,448,480,256,288,320,352,128,160,192,224,0,32,64,96},{385,417,4..., dimensions={0} | all-to-all | bytes 262144 | tf_op jit(solution)/shard_map/all_to_all | solution.py:187
  76.7 0.0 copy-done.1
  76.7 0.0 copy-done.2
  76.7 1.7 %shard_map.64 = (f32[64,256]{1,0:T(8,128)}, bf16[512,2048]{1,0:T(8,128)(2,1)}) custom-call(bf16[16,4,8,128]{3,2,1,0:T(8,128)(2,1)S(1)} %all_to_all.29.refs_0_, bf16[64,256]{1,0:T(8,128)(2,1)S(1)} %copy-done.2, bf16[64,2048]{1,0:T(8,128)(2,1)S(1)} %copy-done.1), custom_call_target="tpu_custom_call" | custom-call | flops 134217728 | bytes 2359296 | tf_op jit(solution)/shard_map/pallas_call | solution.py:106
  (2 shorter events, 0.0 us)
Async XLA Ops:
  0.6 37.3 %copy-start = (bf16[4096,256]{1,0:T(8,128)(2,1)S(1)}, bf16[4096,256]{1,0:T(8,128)(2,1)}, u32[]{:S(2)}) copy-start(bf16[4096,256]{1,0:T(8,128)(2,1)} %param.4) | copy-start | bytes 6291460
  26.3 50.4 %copy-start.1 = (bf16[64,2048]{1,0:T(8,128)(2,1)S(1)}, bf16[64,2048]{1,0:T(8,128)(2,1)}, u32[]{:S(2)}) copy-start(bf16[64,2048]{1,0:T(8,128)(2,1)} %refs_2_.1) | copy-start | bytes 786436
  26.3 50.4 %copy-start.2 = (bf16[64,256]{1,0:T(8,128)(2,1)S(1)}, bf16[64,256]{1,0:T(8,128)(2,1)}, u32[]{:S(2)}) copy-start(bf16[64,256]{1,0:T(8,128)(2,1)} %refs_1_.1) | copy-start | bytes 98308

commit v8 on v7

--- a/solution.py
+++ b/solution.py
@@ -7,7 +7,7 @@
 
 SUB, LANE = 8, 128
 F32, BF16 = jnp.float32, jnp.bfloat16
-ROW_FIRST, COL_FIRST = 12, 26
+ROW_FIRST, COL_FIRST = 13, 26
 PARAMS = pltpu.CompilerParams(vmem_limit_bytes=8 << 20)
 
 

time: 78.8 us -> 78.1 us (level)
  no operation moved by 1% of the time
where the time goes in v8:
time: 78.1 us; the launch traced here: 77.7 us
  blocking collectives  73.9 us (95%)
  Pallas kernels  3.15 us (4%)
    all_to_all x5, blocking collectives, exchange(): return lax.all_to_all(x, axis, 0, 0, tiled=True, axis_index_groups=groups)  73.9 us
    pallas_call x1, Pallas kernels, products(): pl.pallas_call(kernel, in_specs=[pl.BlockSpec(memory_space=pltpu.VMEM)] *...  1.68 us

profile of v8, /device:TPU:1, one launch (start us, length us, event | category | flops | bytes accessed | tf_op | source)
XLA Modules:
  0.0 77.7 jit_solution(3603959915144645616)
XLA Ops:
  0.6 0.0 copy-start
  0.6 0.9 %shard_map.59 = bf16[8,64,128]{2,1,0:T(8,128)(2,1)S(1)} custom-call(bf16[64,128]{1,0:T(8,128)(2,1)} %x_ref.1), custom_call_target="tpu_custom_call" | custom-call | bytes 262144 | tf_op jit(solution)/shard_map/pallas_call | solution.py:138
  1.5 24.7 %all_to_all.25.x_ref = bf16[8,64,128]{2,1,0:T(8,128)(2,1)S(1)} all-to-all(bf16[8,64,128]{2,1,0:T(8,128)(2,1)S(1)} %shard_map.59), channel_id=1, replica_groups={{26,24,30,28,18,16,22,20},{27,25,31,29,19,17,23,21},{10,8,14,12,2,0,6,4..., dimensions={0} | all-to-all | bytes 262144 | tf_op jit(solution)/shard_map/all_to_all | solution.py:187
  26.2 0.1 shard_map.60
  26.3 0.0 copy-start.1
  26.3 0.0 copy-start.2
  26.3 11.6 %all_to_all.26.refs_0_ = bf16[4,8,64,128]{3,2,1,0:T(8,128)(2,1)S(1)} all-to-all(bf16[4,8,64,128]{3,2,1,0:T(8,128)(2,1)S(1)} %shard_map.60), channel_id=1, replica_groups={{26,27,10,11},{24,25,8,9},{30,31,14,15},{28,29,12,13},{18,19,2,3},{16,1..., dimensions={0} | all-to-all | bytes 1048576 | tf_op jit(solution)/shard_map/all_to_all | solution.py:187
  37.9 0.0 copy-done
  37.9 0.5 shard_map.61
  38.4 10.7 %all_to_all.27.tiles_ref = f32[16,8,128]{2,1,0:T(8,128)S(1)} all-to-all(f32[16,8,128]{2,1,0:T(8,128)S(1)} %shard_map.61), channel_id=1, replica_groups={{416,384,480,448,288,256,352,320,160,128,224,192,32,0,96,64},{417,385,4..., dimensions={0} | all-to-all | bytes 131072 | tf_op jit(solution)/shard_map/all_to_all | solution.py:187
  49.1 17.2 %all_to_all.28.refs_0_ = bf16[32,8,128]{2,1,0:T(8,128)(2,1)S(1)} all-to-all(bf16[32,8,128]{2,1,0:T(8,128)(2,1)S(1)} %get-tuple-element.4), channel_id=1, replica_groups={{26,10,18,2,30,14,22,6,24,8,16,0,28,12,20,4,27,11,19,3,31,15,23,7,25,9,..., dimensions={0} | all-to-all | bytes 131072 | tf_op jit(solution)/shard_map/all_to_all | solution.py:187
  66.4 9.6 %all_to_all.29.refs_0_ = bf16[16,4,8,128]{3,2,1,0:T(8,128)(2,1)S(1)} all-to-all(bf16[16,4,8,128]{3,2,1,0:T(8,128)(2,1)S(1)} %shard_map.63), channel_id=1, replica_groups={{416,384,480,448,288,256,352,320,160,128,224,192,32,0,96,64},{417,385,4..., dimensions={0} | all-to-all | bytes 262144 | tf_op jit(solution)/shard_map/all_to_all | solution.py:187
  76.0 0.0 copy-done.1
  76.0 0.0 copy-done.2
  76.0 1.7 %shard_map.64 = (f32[64,256]{1,0:T(8,128)}, bf16[512,2048]{1,0:T(8,128)(2,1)}) custom-call(bf16[16,4,8,128]{3,2,1,0:T(8,128)(2,1)S(1)} %all_to_all.29.refs_0_, bf16[64,256]{1,0:T(8,128)(2,1)S(1)} %copy-done.2, bf16[64,2048]{1,0:T(8,128)(2,1)S(1)} %copy-done.1), custom_call_target="tpu_custom_call" | custom-call | flops 134217728 | bytes 2359296 | tf_op jit(solution)/shard_map/pallas_call | solution.py:106
  (2 shorter events, 0.0 us)
Async XLA Ops:
  0.6 37.3 %copy-start = (bf16[4096,256]{1,0:T(8,128)(2,1)S(1)}, bf16[4096,256]{1,0:T(8,128)(2,1)}, u32[]{:S(2)}) copy-start(bf16[4096,256]{1,0:T(8,128)(2,1)} %param.4) | copy-start | bytes 6291460
  26.3 49.7 %copy-start.1 = (bf16[64,2048]{1,0:T(8,128)(2,1)S(1)}, bf16[64,2048]{1,0:T(8,128)(2,1)}, u32[]{:S(2)}) copy-start(bf16[64,2048]{1,0:T(8,128)(2,1)} %refs_2_.1) | copy-start | bytes 786436
  26.3 49.7 %copy-start.2 = (bf16[64,256]{1,0:T(8,128)(2,1)S(1)}, bf16[64,256]{1,0:T(8,128)(2,1)}, u32[]{:S(2)}) copy-start(bf16[64,256]{1,0:T(8,128)(2,1)} %refs_1_.1) | copy-start | bytes 98308

commit v9 on v8

--- a/solution.py
+++ b/solution.py
@@ -49,12 +49,10 @@
     for t in range(1, tiles_ref.shape[0]):
         pulled = pulled + tiles_ref[t]
     high = pulled.astype(BF16)
-    low = (pulled - high.astype(F32)).astype(BF16)
     for t in range(high_ref.shape[0]):
         high_ref[t] = high
     for t in range(own_ref.shape[0]):
         own_ref[t, 0] = high
-        own_ref[t, 1] = low
 
 
 def reduced(tiles, copies):
@@ -62,14 +60,14 @@
     tile = tiles.shape[1:]
     return pl.pallas_call(
         reduced_kernel,
-        out_shape=[jax.ShapeDtypeStruct((copies,) + tile, BF16), jax.ShapeDtypeStruct((rows, 2) + tile, BF16)],
+        out_shape=[jax.ShapeDtypeStruct((copies,) + tile, BF16), jax.ShapeDtypeStruct((rows, 1) + tile, BF16)],
         compiler_params=PARAMS,
         cost_estimate=pl.CostEstimate(flops=tiles.size, bytes_accessed=10 * tiles.size, transcendentals=0),
     )(tiles)
 
 
 def product_kernel(scale, tiles_ref, direct_ref, panel_ref, factor_ref, out_ref, left_ref, sum_ref, wide_ref, sems):
-    rows, blocks = tiles_ref.shape[0], tiles_ref.shape[1] - 2
+    rows, blocks = tiles_ref.shape[0], tiles_ref.shape[1] - 1
     across = direct_ref.shape[1] // LANE
     chunks = sems.shape[0] - 1
     chunk = out_ref.shape[0] // chunks
@@ -80,7 +78,7 @@
             lane = (b * across + j) * LANE
             left_ref[at, lane : lane + LANE] = tiles_ref[t, b].astype(F32)
         lanes = slice(j * LANE, (j + 1) * LANE)
-        pulled = tiles_ref[t, blocks].astype(F32) + tiles_ref[t, blocks + 1].astype(F32)
+        pulled = tiles_ref[t, blocks].astype(F32)
         sum_ref[at, lanes] = (direct_ref[at, lanes].astype(F32) + pulled) * scale
     copies = [pltpu.make_async_copy(sum_ref, factor_ref, sems.at[chunks])]
     copies[0].start()
@@ -97,7 +95,7 @@
 
 def products(tiles, direct, panel, scale):
     k, columns = panel.shape
-    depth = (tiles.shape[1] - 2) * direct.shape[1]
+    depth = (tiles.shape[1] - 1) * direct.shape[1]
     chunks = 4
 
     def kernel(*refs):

time: 78.1 us -> 77.8 us (level)
  no operation moved by 1% of the time
where the time goes in v9:
time: 77.8 us; the launch traced here: 77.4 us
  blocking collectives  73.6 us (95%)
  Pallas kernels  3.17 us (4%)
    all_to_all x5, blocking collectives, exchange(): return lax.all_to_all(x, axis, 0, 0, tiled=True, axis_index_groups=groups)  73.6 us
    pallas_call x1, Pallas kernels, products(): pl.pallas_call(kernel, in_specs=[pl.BlockSpec(memory_space=pltpu.VMEM)] *...  1.69 us

profile of v9, /device:TPU:1, one launch (start us, length us, event | category | flops | bytes accessed | tf_op | source)
XLA Modules:
  0.0 77.4 jit_solution(5914016463724608837)
XLA Ops:
  0.6 0.0 copy-start
  0.6 0.9 %shard_map.59 = bf16[8,64,128]{2,1,0:T(8,128)(2,1)S(1)} custom-call(bf16[64,128]{1,0:T(8,128)(2,1)} %x_ref.1), custom_call_target="tpu_custom_call" | custom-call | bytes 262144 | tf_op jit(solution)/shard_map/pallas_call | solution.py:136
  1.5 24.7 %all_to_all.25.x_ref = bf16[8,64,128]{2,1,0:T(8,128)(2,1)S(1)} all-to-all(bf16[8,64,128]{2,1,0:T(8,128)(2,1)S(1)} %shard_map.59), channel_id=1, replica_groups={{26,24,30,28,18,16,22,20},{27,25,31,29,19,17,23,21},{10,8,14,12,2,0,6,4..., dimensions={0} | all-to-all | bytes 262144 | tf_op jit(solution)/shard_map/all_to_all | solution.py:185
  26.2 0.1 shard_map.60
  26.3 0.0 copy-start.1
  26.3 0.0 copy-start.2
  26.3 11.6 %all_to_all.26.refs_0_ = bf16[4,8,64,128]{3,2,1,0:T(8,128)(2,1)S(1)} all-to-all(bf16[4,8,64,128]{3,2,1,0:T(8,128)(2,1)S(1)} %shard_map.60), channel_id=1, replica_groups={{26,27,10,11},{24,25,8,9},{30,31,14,15},{28,29,12,13},{18,19,2,3},{16,1..., dimensions={0} | all-to-all | bytes 1048576 | tf_op jit(solution)/shard_map/all_to_all | solution.py:185
  37.9 0.0 copy-done
  37.9 0.5 shard_map.61
  38.4 10.7 %all_to_all.27.tiles_ref = f32[16,8,128]{2,1,0:T(8,128)S(1)} all-to-all(f32[16,8,128]{2,1,0:T(8,128)S(1)} %shard_map.61), channel_id=1, replica_groups={{416,384,480,448,288,256,352,320,160,128,224,192,32,0,96,64},{417,385,4..., dimensions={0} | all-to-all | bytes 131072 | tf_op jit(solution)/shard_map/all_to_all | solution.py:185
  49.1 17.2 %all_to_all.28.refs_0_ = bf16[32,8,128]{2,1,0:T(8,128)(2,1)S(1)} all-to-all(bf16[32,8,128]{2,1,0:T(8,128)(2,1)S(1)} %get-tuple-element.4), channel_id=1, replica_groups={{26,10,18,2,30,14,22,6,24,8,16,0,28,12,20,4,27,11,19,3,31,15,23,7,25,9,..., dimensions={0} | all-to-all | bytes 131072 | tf_op jit(solution)/shard_map/all_to_all | solution.py:185
  66.4 9.4 %all_to_all.29.refs_0_ = bf16[16,3,8,128]{3,2,1,0:T(8,128)(2,1)S(1)} all-to-all(bf16[16,3,8,128]{3,2,1,0:T(8,128)(2,1)S(1)} %shard_map.63), channel_id=1, replica_groups={{416,384,480,448,288,256,352,320,160,128,224,192,32,0,96,64},{417,385,4..., dimensions={0} | all-to-all | bytes 196608 | tf_op jit(solution)/shard_map/all_to_all | solution.py:185
  75.7 0.0 copy-done.1
  75.8 0.0 copy-done.2
  75.8 1.7 %shard_map.64 = (f32[64,256]{1,0:T(8,128)}, bf16[512,2048]{1,0:T(8,128)(2,1)}) custom-call(bf16[16,3,8,128]{3,2,1,0:T(8,128)(2,1)S(1)} %all_to_all.29.refs_0_, bf16[64,256]{1,0:T(8,128)(2,1)S(1)} %copy-done.2, bf16[64,2048]{1,0:T(8,128)(2,1)S(1)} %copy-done.1), custom_call_target="tpu_custom_call" | custom-call | flops 134217728 | bytes 2359296 | tf_op jit(solution)/shard_map/pallas_call | solution.py:104
  (2 shorter events, 0.0 us)
Async XLA Ops:
  0.6 37.3 %copy-start = (bf16[4096,256]{1,0:T(8,128)(2,1)S(1)}, bf16[4096,256]{1,0:T(8,128)(2,1)}, u32[]{:S(2)}) copy-start(bf16[4096,256]{1,0:T(8,128)(2,1)} %param.4) | copy-start | bytes 6291460
  26.3 49.5 %copy-start.1 = (bf16[64,2048]{1,0:T(8,128)(2,1)S(1)}, bf16[64,2048]{1,0:T(8,128)(2,1)}, u32[]{:S(2)}) copy-start(bf16[64,2048]{1,0:T(8,128)(2,1)} %refs_2_.1) | copy-start | bytes 786436
  26.3 49.4 %copy-start.2 = (bf16[64,256]{1,0:T(8,128)(2,1)S(1)}, bf16[64,256]{1,0:T(8,128)(2,1)}, u32[]{:S(2)}) copy-start(bf16[64,256]{1,0:T(8,128)(2,1)} %refs_1_.1) | copy-start | bytes 98308
